TPU v7x, 256 devices: a whole 4x4x8 slice. The times are simulated.
256 devices in a mesh: ta: 16 (over x_hi, z), ha: 16 (over y, x_lo, core).
Axes of the slice: x: 4 (x_hi: 2, x_lo: 2; x = x_hi * 2 + x_lo), y: 4, z: 8, core: 2. Of those that a mesh axis runs over, the one named last changes fastest.
Arguments:
- queries: bfloat16 [16, 64, 32, 1280], P('ta', 'ha'), may hold values from -6 to 6
- keys: bfloat16 [16, 64, 32, 1280], P('ta', 'ha'), may hold values from -6 to 6
- values: bfloat16 [16, 64, 32, 1280], P('ta', 'ha'), may hold values from -6 to 6
- grad_out: bfloat16 [16, 64, 32, 2560], P('ta', 'ha'), may hold values from -6 to 6
- out_weight: bfloat16 [1280, 2560], P(('ta', 'ha')), may hold values from -0.15625 to 0.15625
- windows: int32 [16, 64, 4, 3], P('ta', 'ha'), may hold values from 0 to 1
Outputs:
- grad_query: bfloat16 [16, 64, 32, 1280], P('ta', 'ha')
- grad_key: bfloat16 [16, 64, 32, 1280], P('ta', 'ha')
- grad_value: bfloat16 [16, 64, 32, 1280], P('ta', 'ha')
- weight_grad: float32 [1280, 2560], P(('ta', 'ha'))
All inputs are finite; a program needn't handle non-finite values.
Results may differ from a plain program's by a relative error of at most 0.024.
Values may be sent and summed in bfloat16 or wider, within the bound.
No kernel may reach another device: no remote copies, remote signals or barrier semaphores. Data moves between devices by JAX's collectives and lax.ppermute only.
A program may use at most 128 MiB of HBM per device.

v0:
```python
import jax
import jax.numpy as jnp
from jax import lax
from jax.experimental import pallas as pl
from jax.sharding import Mesh
from jax.sharding import PartitionSpec as P

HEAD_DIM = 64
TILE_W = 8
LANES = 128
NEG = -1e30

MESH_SHAPE = (2, 8, 4, 2, 2)
MESH_NAMES = ("xh", "z", "y", "xl", "c")
TA = ("xh", "z")
HA = ("y", "xl", "c")
XY = ("xh", "xl", "y")
PER_STEP = 5


def shifted(value, axis, steps):
    count = lax.axis_size(axis)
    first, last = (max(0, -steps), min(count, count - steps))
    return lax.ppermute(value, axis, [(source, source + steps) for source in range(first, last)])


def exchanged(blocks, axis):
    return lax.all_to_all(blocks, axis, 0, 0, tiled=True)


def flipped(value, flip_y, flip_core):
    pairs = []
    for y in range(4):
        for c in range(2):
            pairs.append((y * 2 + c, (y ^ flip_y) * 2 + (c ^ flip_core)))
    return lax.ppermute(value, ("y", "c"), pairs)


def gathered_weight(weight):
    width = weight.shape[1]
    rows = exchanged(jnp.broadcast_to(weight[None], (8, *weight.shape)), "z")
    rows = rows.reshape(-1, width)
    halves = jnp.swapaxes(rows.reshape(-1, 2, width // 2), 0, 1)
    blocks = jnp.broadcast_to(halves[None], (8, *halves.shape))
    blocks = blocks.reshape(16, *halves.shape[1:])
    return exchanged(blocks, XY).reshape(-1, width // 2)


def scattered_sum(partial):
    rows, half = partial.shape
    n = rows // 16
    blocks = exchanged(partial.reshape(16, n, half), XY)
    halves = jnp.sum(blocks.reshape(8, 2, n, half).astype(jnp.float32), axis=0)
    both = jnp.concatenate([halves[0], halves[1]], axis=1).astype(jnp.bfloat16)
    blocks = exchanged(both.reshape(8, n // 8, 2 * half), "z")
    return jnp.sum(blocks.astype(jnp.float32), axis=0)


def row_order(own_rows):
    c = lax.axis_index("c")
    shape = (2, 4, 4, 8, own_rows)
    core = (c + lax.broadcasted_iota(jnp.int32, shape, 0)) % 2
    x = lax.broadcasted_iota(jnp.int32, shape, 1)
    y = lax.broadcasted_iota(jnp.int32, shape, 2)
    z = lax.broadcasted_iota(jnp.int32, shape, 3)
    row = lax.broadcasted_iota(jnp.int32, shape, 4)
    number = ((x // 2) * 8 + z) * 16 + y * 4 + (x % 2) * 2 + core
    return (number * own_rows + row).reshape(-1)


def key_places(row_count, col_count):
    centre = (3, row_count, col_count)
    edges = (2, 3, col_count)

    def joined(first, second):
        return jnp.concatenate([first.reshape(-1), second.reshape(-1)])

    iota = lax.broadcasted_iota
    frame = joined(iota(jnp.int32, centre, 0), iota(jnp.int32, edges, 1)) - 1
    edge_row = iota(jnp.int32, edges, 0) * (row_count + 1) - 1
    row = joined(iota(jnp.int32, centre, 1), edge_row)
    tile = joined(iota(jnp.int32, centre, 2), iota(jnp.int32, edges, 2)) // TILE_W
    return frame, row, tile


def visible_keys(windows, frames_in_all, rows_in_all, row_count, col_count):
    time_index = lax.axis_index(TA)
    first_row = lax.axis_index(HA) * row_count
    tokens = row_count * col_count
    extent = jnp.repeat(windows[0], TILE_W, axis=1).reshape(tokens, 3)
    frame, row, tile = key_places(row_count, col_count)
    query = lax.broadcasted_iota(jnp.int32, (1, tokens), 1)
    inside = (
        (frame + time_index >= 0)
        & (frame + time_index < frames_in_all)
        & (row + first_row >= 0)
        & (row + first_row < rows_in_all)
    )[:, None]
    query_row = query // col_count
    query_tile = query % col_count // TILE_W
    inside = inside & (jnp.abs(frame)[:, None] <= extent[None, :, 0])
    inside = inside & (jnp.abs(row[:, None] - query_row) <= extent[None, :, 1])
    inside = inside & (jnp.abs(tile[:, None] - query_tile) <= extent[None, :, 2])
    return jnp.where(inside, 0.0, NEG).astype(jnp.float32)


def stacked(pair):
    lane = lax.broadcasted_iota(jnp.int32, pair.shape, 1)
    zero = jnp.zeros_like(pair)
    return jnp.concatenate(
        [jnp.where(lane < HEAD_DIM, pair, zero), jnp.where(lane < HEAD_DIM, zero, pair)], axis=0
    )


def unstacked(both):
    n = both.shape[0] // 2
    lane = lax.broadcasted_iota(jnp.int32, (n, LANES), 1)
    return jnp.where(lane < HEAD_DIM, both[:n], both[n:])


def dot(a, b, a_dim, b_dim):
    return lax.dot_general(
        a, b, (((a_dim,), (b_dim,)), ((), ())), preferred_element_type=jnp.float32
    )


def near(refs, which, lanes):
    return jnp.concatenate([ref[which, :, lanes] for ref in refs], axis=0)


def scaled_queries(q_ref, lanes):
    return stacked(q_ref[:, lanes] * jnp.asarray(HEAD_DIM**-0.5, jnp.bfloat16))


def attend_kernel(q_ref, *refs):
    near_refs = refs[:5]
    bias_ref, out_ref, total_ref = refs[5:]
    for i in range(PER_STEP):
        lanes = slice(i * LANES, (i + 1) * LANES)
        queries = scaled_queries(q_ref, lanes)
        scores = dot(near(near_refs, 0, lanes), queries, 1, 1)
        bias = bias_ref[...]
        scores = scores + jnp.concatenate([bias, bias], axis=1)
        top = jnp.max(scores, axis=0, keepdims=True)
        raised = jnp.exp(scores - top)
        total = jnp.sum(raised, axis=0, keepdims=True)
        total_ref[i] = jnp.broadcast_to(top + jnp.log(total), total_ref.shape[1:])
        mixed = dot(near(near_refs, 1, lanes), raised.astype(jnp.bfloat16), 0, 0) / total
        out_ref[:, lanes] = unstacked(mixed.T).astype(jnp.bfloat16)


def grads_kernel(q_ref, g_ref, total_ref, *refs):
    near_refs = refs[:5]
    bias_ref, dq_ref = refs[5:7]
    out_refs = refs[7:]
    for i in range(PER_STEP):
        lanes = slice(i * LANES, (i + 1) * LANES)
        queries = scaled_queries(q_ref, lanes)
        grads = stacked(g_ref[:, lanes])
        keys = near(near_refs, 0, lanes)
        bias = bias_ref[...]
        scores = dot(keys, queries, 1, 1) + jnp.concatenate([bias, bias], axis=1)
        weights = jnp.exp(scores - total_ref[i, 0:1, :])
        dweights = weights * dot(near(near_refs, 1, lanes), grads, 1, 1)
        delta = jnp.sum(dweights, axis=0, keepdims=True)
        dscores = (dweights - weights * delta).astype(jnp.bfloat16)
        dvalues = dot(weights.astype(jnp.bfloat16), grads, 1, 0)
        dkeys = dot(dscores, queries, 1, 0)
        dqueries = dot(keys, dscores, 0, 0) * HEAD_DIM**-0.5
        dq_ref[:, lanes] = unstacked(dqueries.T).astype(jnp.bfloat16)
        first = 0
        for ref in out_refs:
            last = first + ref.shape[1]
            ref[0, :, lanes] = dkeys[first:last].astype(jnp.bfloat16)
            ref[1, :, lanes] = dvalues[first:last].astype(jnp.bfloat16)
            first = last


def specs(tokens, nearby, bias):
    width = PER_STEP * LANES
    by_pair = pl.BlockSpec((tokens, width), lambda j: (0, j))
    near_specs = [pl.BlockSpec((*x.shape[:2], width), lambda j: (0, 0, j)) for x in nearby]
    totals = pl.BlockSpec((PER_STEP, 8, 2 * tokens), lambda j: (j, 0, 0))
    return by_pair, near_specs, totals, pl.BlockSpec(bias.shape, lambda j: (0, 0))


def attend(queries, nearby, bias):
    tokens, inner = queries.shape
    keys = bias.shape[0]
    by_pair, near_specs, totals, bias_spec = specs(tokens, nearby, bias)
    return pl.pallas_call(
        attend_kernel,
        grid=(inner // LANES // PER_STEP,),
        in_specs=[by_pair, *near_specs, bias_spec],
        out_specs=[by_pair, totals],
        out_shape=[
            jax.ShapeDtypeStruct((tokens, inner), jnp.bfloat16),
            jax.ShapeDtypeStruct((inner // LANES, 8, 2 * tokens), jnp.float32),
        ],
        cost_estimate=pl.CostEstimate(
            flops=8 * keys * tokens * inner, bytes_accessed=4 * keys * inner,
            transcendentals=keys * tokens * 20),
        name="attend",
    )(queries, *nearby, bias)


def attention_grads(queries, grads, totals, nearby, bias):
    tokens, inner = queries.shape
    keys = bias.shape[0]
    by_pair, near_specs, totals_spec, bias_spec = specs(tokens, nearby, bias)
    return pl.pallas_call(
        grads_kernel,
        grid=(inner // LANES // PER_STEP,),
        in_specs=[by_pair, by_pair, totals_spec, *near_specs, bias_spec],
        out_specs=[by_pair, *near_specs],
        out_shape=[jax.ShapeDtypeStruct((tokens, inner), jnp.bfloat16)]
        + [jax.ShapeDtypeStruct(x.shape, jnp.bfloat16) for x in nearby],
        cost_estimate=pl.CostEstimate(
            flops=20 * keys * tokens * inner, bytes_accessed=8 * keys * inner,
            transcendentals=keys * tokens * 20),
        name="attention_grads",
    )(queries, grads, totals, *nearby, bias)


def step(queries, keys, values, grad_out, out_weight, windows):
    frames, row_count, col_count, inner = queries.shape
    model_width = grad_out.shape[3]
    tokens = frames * row_count * col_count
    all_frames = frames * lax.axis_size(TA)
    all_rows = row_count * lax.axis_size(HA)
    total_tokens = all_frames * all_rows * col_count
    flat_queries = queries.reshape(tokens, inner)
    flat_grad = grad_out.reshape(tokens, model_width)

    own = jnp.stack([keys.reshape(tokens, inner), values.reshape(tokens, inner)])
    centre = (shifted(own, TA, 1), own, shifted(own, TA, -1))
    top = jnp.concatenate([x[:, :col_count] for x in centre], axis=1)
    bottom = jnp.concatenate([x[:, tokens - col_count :] for x in centre], axis=1)
    nearby = (*centre, shifted(bottom, HA, 1), shifted(top, HA, -1))

    wide_half = model_width // 2
    odd = lax.axis_index("y") % 2
    from_pair = flipped(
        lax.dynamic_slice_in_dim(flat_grad, (1 - odd) * wide_half, wide_half, axis=1), 1, 0
    )
    mine = lax.dynamic_slice_in_dim(flat_grad, odd * wide_half, wide_half, axis=1)
    mine = jnp.stack([mine, from_pair])
    others = flipped(mine, 0, 1)
    group_grad = jnp.stack([mine, others], axis=1).reshape(4 * tokens, wide_half)

    weight = gathered_weight(out_weight)
    order = row_order(out_weight.shape[0])
    picks = (order[:, None] == lax.broadcasted_iota(jnp.int32, (1, inner), 1)).astype(jnp.bfloat16)
    bias = visible_keys(windows, all_frames, all_rows, row_count, col_count)

    attended, totals = attend(flat_queries, nearby, bias)
    picked = dot(attended, picks, 1, 1).astype(jnp.bfloat16)
    half = inner // 2
    group_attended = jnp.concatenate(
        [picked[:, :half], flipped(picked[:, half:], 0, 1),
         flipped(picked[:, :half], 1, 0), flipped(picked[:, half:], 1, 1)], axis=0
    )
    partial = dot(group_attended, group_grad, 0, 0) * total_tokens ** (-0.5)
    partial = partial.astype(jnp.bfloat16)
    weight_grad = scattered_sum(partial)

    group_attn = dot(group_grad, weight, 1, 1)
    sent = group_attn.astype(jnp.bfloat16)
    here_other = flipped(sent[tokens : 2 * tokens], 0, 1)
    pair_own = flipped(sent[2 * tokens : 3 * tokens], 1, 0)
    pair_other = flipped(sent[3 * tokens :], 1, 1)
    own_half = group_attn[:tokens] + pair_own.astype(jnp.float32)
    other_half = here_other.astype(jnp.float32) + pair_other.astype(jnp.float32)
    split_attn = jnp.concatenate([own_half, other_half], axis=1).astype(jnp.bfloat16)
    grad_attn = dot(split_attn, picks, 1, 0).astype(jnp.bfloat16)

    query_grad, *pieces = attention_grads(flat_queries, grad_attn, totals, nearby, bias)
    to_bottom = shifted(pieces[3], HA, -1).astype(jnp.float32)
    to_top = shifted(pieces[4], HA, 1).astype(jnp.float32)
    rest = jnp.zeros_like(pieces[0][:, : tokens - col_count], jnp.float32)

    def with_edges(i):
        at = slice(i * col_count, (i + 1) * col_count)
        return (pieces[i].astype(jnp.float32)
                + jnp.concatenate([to_top[:, at], rest], axis=1)
                + jnp.concatenate([rest, to_bottom[:, at]], axis=1))

    before, here, after = [with_edges(i) for i in range(3)]
    before = shifted(before.astype(jnp.bfloat16), TA, -1)
    after = shifted(after.astype(jnp.bfloat16), TA, 1)
    total = (here + before.astype(jnp.float32) + after.astype(jnp.float32)).astype(jnp.bfloat16)
    return (
        query_grad.reshape(queries.shape),
        total[0].reshape(queries.shape),
        total[1].reshape(queries.shape),
        weight_grad,
    )


def solution(mesh):
    fine = Mesh(mesh.devices.reshape(MESH_SHAPE), MESH_NAMES)
    tokens = P(TA, HA, None, None)
    rows = P(TA + HA, None)
    return jax.shard_map(
        step,
        mesh=fine,
        in_specs=(tokens, tokens, tokens, tokens, rows, tokens),
        out_specs=(tokens, tokens, tokens, rows),
        check_vma=False,
    )
```

profile of v0, /device:TPU:25, one launch (start us, length us, event | category | flops | bytes accessed | tf_op | source)
XLA Modules:
  0.0 194.0 jit_solution(17641231998888466770)
XLA Ops:
  3.3 5.0 %collective-permute-start.5 = (bf16[2,128,1280]{2,1,0:T(8,128)(2,1)S(1)}, bf16[2,128,1280]{2,1,0:T(8,128)(2,1)}, u32[]{:S(2)}, u32[]{:S(2)}) collective-permute-start(bf16[2,128,1280]{2,1,0:T(8,128)(2,1)S(1)} %pad_maximum_fusion.1.refs_1_), channel_id=1, source_target_pairs={{0,16},{16,32},{32,48},{48,64},{64,80},{80,96},{96,112},{112,128},... | collective-permute-start | bytes 1966088 | tf_op jit(solution)/shard_map/ppermute | solution.py:24
  9.1 9.4 %all-to-all-start = ((bf16[8,5,2560]{2,1,0:T(8,128)(2,1)}), bf16[8,5,2560]{2,1,0:T(8,128)(2,1)S(1)}, u32[]{:S(2)}, u32[]{:S(2)}) async-start(bf16[8,5,2560]{2,1,0:T(8,128)(2,1)} %broadcast_in_dim.12), calls=%async_computation | async-start | bytes 655360 | tf_op jit(solution)/shard_map/all_to_all | solution.py:28
  22.4 4.1 %collective-permute-done = bf16[128,1280]{1,0:T(8,128)(2,1)S(1)} collective-permute-done((bf16[128,1280]{1,0:T(8,128)(2,1)S(1)}, bf16[128,1280]{1,0:T(8,128)(2,1)S(1)}, u32[]{:S(2)}, u32[]{:S(2)}) %collective-permute-start) | collective-permute-done | bytes 327712 | tf_op jit(solution)/shard_map/ppermute | solution.py:36
  27.4 2.4 %collective-permute-start.1 = (bf16[2,128,1280]{2,1,0:T(8,128)(2,1)}, bf16[2,128,1280]{2,1,0:T(8,128)(2,1)}, u32[]{:S(2)}, u32[]{:S(2)}) collective-permute-start(bf16[2,128,1280]{2,1,0:T(8,128)(2,1)} %get-tuple-element.32), channel_id=1, source_target_pairs={{0,1},{1,0},{4,5},{5,4},{8,9},{9,8},{12,13},{13,12},{2,3},{3,2},{6... | collective-permute-start | bytes 1966088 | tf_op jit(solution)/shard_map/ppermute | solution.py:36
  29.8 7.3 %all-to-all-done = bf16[8,5,2560]{2,1,0:T(8,128)(2,1)S(1)} async-done(((bf16[8,5,2560]{2,1,0:T(8,128)(2,1)}), bf16[8,5,2560]{2,1,0:T(8,128)(2,1)S(1)}, u32[]{:S(2)}, u32[]{:S(2)}) %all-to-all-start) | async-done | bytes 204832 | tf_op jit(solution)/shard_map/all_to_all | solution.py:28
  38.5 5.1 %all-to-all-start.1 = ((bf16[16,40,1280]{2,1,0:T(8,128)(2,1)}), bf16[16,40,1280]{2,1,0:T(8,128)(2,1)S(1)}, u32[]{:S(2)}, u32[]{:S(2)}) async-start(bf16[16,40,1280]{2,1,0:T(8,128)(2,1)} %bitcast.9), calls=%async_computation.1 | async-start | bytes 3276800 | tf_op jit(solution)/shard_map/all_to_all | solution.py:28
  45.7 5.6 %collective-permute-start.7 = (bf16[2,96,1280]{2,1,0:T(8,128)(2,1)S(1)}, bf16[2,96,1280]{2,1,0:T(8,128)(2,1)S(1)}, u32[]{:S(2)}, u32[]{:S(2)}) collective-permute-start(bf16[2,96,1280]{2,1,0:T(8,128)(2,1)S(1)} %pad_maximum_fusion.3), channel_id=1, source_target_pairs={{0,1},{1,2},{2,3},{3,4},{4,5},{5,6},{6,7},{7,8},{8,9},{9,10},{10,1... | collective-permute-start | bytes 1474568 | tf_op jit(solution)/shard_map/ppermute | solution.py:24
  53.4 2.3 %pad_maximum_fusion = bf16[2,2,128,1280]{3,2,1,0:T(8,128)(2,1)} fusion(bf16[2,1,128,1280]{3,2,1,0:T(8,128)(2,1)} %bitcast.6, bf16[2,1,128,1280]{3,2,1,0:T(8,128)(2,1)S(1)} %get-tuple-element.31), kind=kLoop, calls=%fused_computation.9 | loop fusion | flops 655360 | bytes 2621440 | tf_op jit(solution)/shard_map/stack | solution.py:249
  55.7 14.0 %collective-permute-done.7.refs_3_ = bf16[2,96,1280]{2,1,0:T(8,128)(2,1)S(1)} collective-permute-done((bf16[2,96,1280]{2,1,0:T(8,128)(2,1)S(1)}, bf16[2,96,1280]{2,1,0:T(8,128)(2,1)S(1)}, u32[]{:S(2)}, u32[]{:S(2)}) %collective-permute-start.7) | collective-permute-done | bytes 491552 | tf_op jit(solution)/shard_map/ppermute | solution.py:24
  70.7 7.4 %attend.1 = (bf16[128,1280]{1,0:T(8,128)(2,1)}, f32[10,8,256]{2,1,0:T(8,128)}) custom-call(bf16[128,1280]{1,0:T(8,128)(2,1)} %bitcast.51, bf16[2,128,1280]{2,1,0:T(8,128)(2,1)} %collective-permute-done.5.refs_0_, bf16[2,128,1280]{2,1,0:T(8,128)(2,1)} %copy-done, bf16[2,128,1280]{2,1,0:T(8,128)(2,1)} %collective-permute-done.6.refs_2_, ...), custom_call_target="tpu_custom_call" | custom-call | flops 754974720 | bytes 2949120 | tf_op jit(solution)/shard_map/attend/pallas_call | solution.py:191
  78.1 2.6 %fusion.41 = (bf16[512,640]{1,0:T(8,128)(2,1)S(1)}, f32[512,640]{1,0:T(8,128)S(1)}) fusion(bf16[512,1280]{1,0:T(8,128)(2,1)} %bitcast.43, bf16[640,1280]{1,0:T(8,128)(2,1)S(1)} %bitcast.41), kind=kOutput, calls=%fused_computation.100 | convolution fusion | flops 839188480 | bytes 4915200 | tf_op jit(solution)/shard_map/dot_general | solution.py:122
  80.8 6.9 %collective-permute-start.2 = (bf16[128,640]{1,0:T(8,128)(2,1)S(1)}, bf16[128,640]{1,0:T(8,128)(2,1)S(1)}, u32[]{:S(2)}, u32[]{:S(2)}) collective-permute-start(bf16[128,640]{1,0:T(8,128)(2,1)S(1)} %get-tuple-element.28), channel_id=1, source_target_pairs={{0,4},{1,5},{4,0},{5,1},{8,12},{9,13},{12,8},{13,9},{2,6},{3,7},{6... | collective-permute-start | bytes 491528 | tf_op jit(solution)/shard_map/ppermute | solution.py:36
  89.8 2.1 %collective-permute-done.2 = bf16[128,640]{1,0:T(8,128)(2,1)S(1)} collective-permute-done((bf16[128,640]{1,0:T(8,128)(2,1)S(1)}, bf16[128,640]{1,0:T(8,128)(2,1)S(1)}, u32[]{:S(2)}, u32[]{:S(2)}) %collective-permute-start.2) | collective-permute-done | bytes 163872 | tf_op jit(solution)/shard_map/ppermute | solution.py:36
  91.9 3.5 %collective-permute-done.4 = bf16[128,640]{1,0:T(8,128)(2,1)S(1)} collective-permute-done((bf16[128,640]{1,0:T(8,128)(2,1)S(1)}, bf16[128,640]{1,0:T(8,128)(2,1)S(1)}, u32[]{:S(2)}, u32[]{:S(2)}) %collective-permute-start.4) | collective-permute-done | bytes 163872 | tf_op jit(solution)/shard_map/ppermute | solution.py:36
  95.4 2.3 %fusion.5.g_ref = bf16[128,1280]{1,0:T(8,128)(2,1)} fusion(s32[1280]{0:T(1024)S(1)} %fusion.26, bf16[128,640]{1,0:T(8,128)(2,1)S(1)} %add_convert_fusion.3, bf16[128,640]{1,0:T(8,128)(2,1)S(1)} %fusion.14), kind=kOutput, calls=%fused_computation.7 | convolution fusion | flops 421888000 | bytes 660480 | tf_op jit(solution)/shard_map/dot_general | solution.py:122
  97.7 8.4 %attention_grads.1 = (bf16[128,1280]{1,0:T(8,128)(2,1)}, bf16[2,128,1280]{2,1,0:T(8,128)(2,1)}, bf16[2,128,1280]{2,1,0:T(8,128)(2,1)}, bf16[2,128,1280]{2,1,0:T(...) custom-call(bf16[128,1280]{1,0:T(8,128)(2,1)} %bitcast.52, bf16[128,1280]{1,0:T(8,128)(2,1)} %fusion.5.g_ref, ...), custom_call_target="tpu_custom_call" | custom-call | flops 1887436800 | bytes 5898240 | tf_op jit(solution)/shard_map/attention_grads/pallas_call | solution.py:211
  110.3 8.4 %collective-permute-done.14 = bf16[128,640]{1,0:T(8,128)(2,1)S(1)} collective-permute-done((bf16[128,640]{1,0:T(8,128)(2,1)S(1)}, bf16[128,640]{1,0:T(8,128)(2,1)S(1)}, u32[]{:S(2)}, u32[]{:S(2)}) %collective-permute-start.14) | collective-permute-done | bytes 163872 | tf_op jit(solution)/shard_map/ppermute | solution.py:36
  118.7 4.2 %collective-permute-done.15 = bf16[128,640]{1,0:T(8,128)(2,1)S(1)} collective-permute-done((bf16[128,640]{1,0:T(8,128)(2,1)S(1)}, bf16[128,640]{1,0:T(8,128)(2,1)S(1)}, u32[]{:S(2)}, u32[]{:S(2)}) %collective-permute-start.15) | collective-permute-done | bytes 163872 | tf_op jit(solution)/shard_map/ppermute | solution.py:36
  122.9 2.2 %fusion.4 = bf16[640,1280]{1,0:T(8,128)(2,1)} fusion(bf16[512,1280]{1,0:T(8,128)(2,1)S(1)} %bitcast.44, bf16[128,640]{1,0:T(8,128)(2,1)S(1)} %collective-permute-done.15, bf16[128,640]{1,0:T(8,128)(2,1)S(1)} %collective-permute-done.14, bf16[128,640]{1,0:T(8,128)(2,1)S(1)} %collective-permute-done.13, bf16[128,640]{1,0:T(8,128)(2,1)S(1)} %get-tuple-element.41), kind=kOutput, calls=%fused_computation.6 | convolution fusion | flops 843120640 | bytes 3604480 | tf_op jit(solution)/shard_map/dot_general | solution.py:122
  125.1 6.0 %all-to-all-start.2 = ((bf16[16,40,1280]{2,1,0:T(8,128)(2,1)}), bf16[16,40,1280]{2,1,0:T(8,128)(2,1)S(1)}, u32[]{:S(2)}, u32[]{:S(2)}) async-start(bf16[16,40,1280]{2,1,0:T(8,128)(2,1)} %bitcast.42), calls=%async_computation.2 | async-start | bytes 3276800 | tf_op jit(solution)/shard_map/all_to_all | solution.py:28
  131.1 2.9 %collective-permute-start.10 = (bf16[2,96,1280]{2,1,0:T(8,128)(2,1)S(1)}, bf16[2,96,1280]{2,1,0:T(8,128)(2,1)S(1)}, u32[]{:S(2)}, u32[]{:S(2)}) collective-permute-start(bf16[2,96,1280]{2,1,0:T(8,128)(2,1)S(1)} %copy-done.12), channel_id=1, source_target_pairs={{1,0},{2,1},{3,2},{4,3},{5,4},{6,5},{7,6},{8,7},{9,8},{10,9},{11,1... | collective-permute-start | bytes 1474568 | tf_op jit(solution)/shard_map/ppermute | solution.py:24
  134.0 29.7 %collective-permute-done.10 = bf16[2,96,1280]{2,1,0:T(8,128)(2,1)S(1)} collective-permute-done((bf16[2,96,1280]{2,1,0:T(8,128)(2,1)S(1)}, bf16[2,96,1280]{2,1,0:T(8,128)(2,1)S(1)}, u32[]{:S(2)}, u32[]{:S(2)}) %collective-permute-start.10) | collective-permute-done | bytes 491552 | tf_op jit(solution)/shard_map/ppermute | solution.py:24
  167.0 4.8 %collective-permute-start.12 = (bf16[2,128,1280]{2,1,0:T(8,128)(2,1)}, bf16[2,128,1280]{2,1,0:T(8,128)(2,1)}, u32[]{:S(2)}, u32[]{:S(2)}) collective-permute-start(bf16[2,128,1280]{2,1,0:T(8,128)(2,1)} %add_convert_fusion.1), channel_id=1, source_target_pairs={{0,16},{16,32},{32,48},{48,64},{64,80},{80,96},{96,112},{112,128},... | collective-permute-start | bytes 1966088 | tf_op jit(solution)/shard_map/ppermute | solution.py:24
  172.3 18.5 %all_to_all.20 = bf16[8,5,2560]{2,1,0:T(8,128)(2,1)S(1)} all-to-all(bf16[8,5,2560]{2,1,0:T(8,128)(2,1)S(1)} %pad_maximum_fusion.5), channel_id=1, replica_groups=mesh['xh'=2,'z'=8,'y'=4,'xl'=2,'c'=2] {'z'}, dimensions={0} | all-to-all | bytes 409600 | tf_op jit(solution)/shard_map/all_to_all | solution.py:28
  (116 shorter events, 27.6 us)
Async XLA Ops:
  0.6 17.9 %copy-start.4 = (bf16[1,4,32,2560]{3,2,1,0:T(8,128)(2,1)S(1)}, bf16[1,4,32,2560]{3,2,1,0:T(8,128)(2,1)}, u32[]{:S(2)}) copy-start(bf16[1,4,32,2560]{3,2,1,0:T(8,128)(2,1)} %param.9) | copy-start | bytes 1966084
  1.9 17.5 %copy-start = (bf16[2,128,1280]{2,1,0:T(8,128)(2,1)}, bf16[2,128,1280]{2,1,0:T(8,128)(2,1)S(1)}, u32[]{:S(2)}) copy-start(bf16[2,128,1280]{2,1,0:T(8,128)(2,1)S(1)} %pad_maximum_fusion.1.refs_1_) | copy-start | bytes 1966084
  1.9 41.7 %collective-permute-start.6 = (bf16[2,128,1280]{2,1,0:T(8,128)(2,1)S(1)}, bf16[2,128,1280]{2,1,0:T(8,128)(2,1)}, u32[]{:S(2)}, u32[]{:S(2)}) collective-permute-start(bf16[2,128,1280]{2,1,0:T(8,128)(2,1)S(1)} %pad_maximum_fusion.1.refs_1_), channel_id=1, source_target_pairs={{16,0},{32,16},{48,32},{64,48},{80,64},{96,80},{112,96},{128,112},... | collective-permute-start | bytes 1966088 | tf_op jit(solution)/shard_map/ppermute | solution.py:24
  3.3 41.3 %collective-permute-start.5 = (bf16[2,128,1280]{2,1,0:T(8,128)(2,1)S(1)}, bf16[2,128,1280]{2,1,0:T(8,128)(2,1)}, u32[]{:S(2)}, u32[]{:S(2)}) collective-permute-start(bf16[2,128,1280]{2,1,0:T(8,128)(2,1)S(1)} %pad_maximum_fusion.1.refs_1_), channel_id=1, source_target_pairs={{0,16},{16,32},{32,48},{48,64},{64,80},{80,96},{96,112},{112,128},... | collective-permute-start | bytes 1966088 | tf_op jit(solution)/shard_map/ppermute | solution.py:24
  9.1 28.0 %all-to-all-start = ((bf16[8,5,2560]{2,1,0:T(8,128)(2,1)}), bf16[8,5,2560]{2,1,0:T(8,128)(2,1)S(1)}, u32[]{:S(2)}, u32[]{:S(2)}) async-start(bf16[8,5,2560]{2,1,0:T(8,128)(2,1)} %broadcast_in_dim.12), calls=%async_computation | async-start | bytes 655360 | tf_op jit(solution)/shard_map/all_to_all | solution.py:28
  18.6 7.8 %collective-permute-start = (bf16[128,1280]{1,0:T(8,128)(2,1)S(1)}, bf16[128,1280]{1,0:T(8,128)(2,1)S(1)}, u32[]{:S(2)}, u32[]{:S(2)}) collective-permute-start(bf16[128,1280]{1,0:T(8,128)(2,1)S(1)} %get-tuple-element.34), channel_id=1, source_target_pairs={{0,4},{1,5},{4,0},{5,1},{8,12},{9,13},{12,8},{13,9},{2,6},{3,7},{6... | collective-permute-start | bytes 983048 | tf_op jit(solution)/shard_map/ppermute | solution.py:36
  27.4 26.0 %collective-permute-start.1 = (bf16[2,128,1280]{2,1,0:T(8,128)(2,1)}, bf16[2,128,1280]{2,1,0:T(8,128)(2,1)}, u32[]{:S(2)}, u32[]{:S(2)}) collective-permute-start(bf16[2,128,1280]{2,1,0:T(8,128)(2,1)} %get-tuple-element.32), channel_id=1, source_target_pairs={{0,1},{1,0},{4,5},{5,4},{8,9},{9,8},{12,13},{13,12},{2,3},{3,2},{6... | collective-permute-start | bytes 1966088 | tf_op jit(solution)/shard_map/ppermute | solution.py:36
  38.5 39.6 %all-to-all-start.1 = ((bf16[16,40,1280]{2,1,0:T(8,128)(2,1)}), bf16[16,40,1280]{2,1,0:T(8,128)(2,1)S(1)}, u32[]{:S(2)}, u32[]{:S(2)}) async-start(bf16[16,40,1280]{2,1,0:T(8,128)(2,1)} %bitcast.9), calls=%async_computation.1 | async-start | bytes 3276800 | tf_op jit(solution)/shard_map/all_to_all | solution.py:28
  45.7 24.0 %collective-permute-start.7 = (bf16[2,96,1280]{2,1,0:T(8,128)(2,1)S(1)}, bf16[2,96,1280]{2,1,0:T(8,128)(2,1)S(1)}, u32[]{:S(2)}, u32[]{:S(2)}) collective-permute-start(bf16[2,96,1280]{2,1,0:T(8,128)(2,1)S(1)} %pad_maximum_fusion.3), channel_id=1, source_target_pairs={{0,1},{1,2},{2,3},{3,4},{4,5},{5,6},{6,7},{7,8},{8,9},{9,10},{10,1... | collective-permute-start | bytes 1474568 | tf_op jit(solution)/shard_map/ppermute | solution.py:24
  51.4 18.3 %collective-permute-start.8 = (bf16[2,96,1280]{2,1,0:T(8,128)(2,1)S(1)}, bf16[2,96,1280]{2,1,0:T(8,128)(2,1)S(1)}, u32[]{:S(2)}, u32[]{:S(2)}) collective-permute-start(bf16[2,96,1280]{2,1,0:T(8,128)(2,1)S(1)} %pad_maximum_fusion.4), channel_id=1, source_target_pairs={{1,0},{2,1},{3,2},{4,3},{5,4},{6,5},{7,6},{8,7},{9,8},{10,9},{11,1... | collective-permute-start | bytes 1474568 | tf_op jit(solution)/shard_map/ppermute | solution.py:24
  80.8 11.1 %collective-permute-start.2 = (bf16[128,640]{1,0:T(8,128)(2,1)S(1)}, bf16[128,640]{1,0:T(8,128)(2,1)S(1)}, u32[]{:S(2)}, u32[]{:S(2)}) collective-permute-start(bf16[128,640]{1,0:T(8,128)(2,1)S(1)} %get-tuple-element.28), channel_id=1, source_target_pairs={{0,4},{1,5},{4,0},{5,1},{8,12},{9,13},{12,8},{13,9},{2,6},{3,7},{6... | collective-permute-start | bytes 491528 | tf_op jit(solution)/shard_map/ppermute | solution.py:36
  89.3 6.1 %collective-permute-start.4 = (bf16[128,640]{1,0:T(8,128)(2,1)S(1)}, bf16[128,640]{1,0:T(8,128)(2,1)S(1)}, u32[]{:S(2)}, u32[]{:S(2)}) collective-permute-start(bf16[128,640]{1,0:T(8,128)(2,1)S(1)} %get-tuple-element.29), channel_id=1, source_target_pairs={{0,5},{1,4},{4,1},{5,0},{8,13},{9,12},{12,9},{13,8},{2,7},{3,6},{6... | collective-permute-start | bytes 491528 | tf_op jit(solution)/shard_map/ppermute | solution.py:36
  89.3 6.0 %collective-permute-start.3 = (bf16[128,640]{1,0:T(8,128)(2,1)S(1)}, bf16[128,640]{1,0:T(8,128)(2,1)S(1)}, u32[]{:S(2)}, u32[]{:S(2)}) collective-permute-start(bf16[128,640]{1,0:T(8,128)(2,1)S(1)} %get-tuple-element.30), channel_id=1, source_target_pairs={{0,1},{1,0},{4,5},{5,4},{8,9},{9,8},{12,13},{13,12},{2,3},{3,2},{6... | collective-permute-start | bytes 491528 | tf_op jit(solution)/shard_map/ppermute | solution.py:36
  97.7 25.2 %copy-start.1 = (bf16[2,2,128,1280]{3,2,1,0:T(8,128)(2,1)S(1)}, bf16[2,2,128,1280]{3,2,1,0:T(8,128)(2,1)}, u32[]{:S(2)}) copy-start(bf16[2,2,128,1280]{3,2,1,0:T(8,128)(2,1)} %pad_maximum_fusion) | copy-start | bytes 3932164
  106.1 27.8 %collective-permute-start.9 = (bf16[2,96,1280]{2,1,0:T(8,128)(2,1)}, bf16[2,96,1280]{2,1,0:T(8,128)(2,1)S(1)}, u32[]{:S(2)}, u32[]{:S(2)}) collective-permute-start(bf16[2,96,1280]{2,1,0:T(8,128)(2,1)} %get-tuple-element.15), channel_id=1, source_target_pairs={{0,1},{1,2},{2,3},{3,4},{4,5},{5,6},{6,7},{7,8},{8,9},{9,10},{10,1... | collective-permute-start | bytes 1474568 | tf_op jit(solution)/shard_map/ppermute | solution.py:24
  108.1 10.6 %collective-permute-start.14 = (bf16[128,640]{1,0:T(8,128)(2,1)S(1)}, bf16[128,640]{1,0:T(8,128)(2,1)S(1)}, u32[]{:S(2)}, u32[]{:S(2)}) collective-permute-start(bf16[128,640]{1,0:T(8,128)(2,1)S(1)} %get-tuple-element.41), channel_id=1, source_target_pairs={{0,4},{1,5},{4,0},{5,1},{8,12},{9,13},{12,8},{13,9},{2,6},{3,7},{6... | collective-permute-start | bytes 491528 | tf_op jit(solution)/shard_map/ppermute | solution.py:36
  108.5 14.4 %collective-permute-start.15 = (bf16[128,640]{1,0:T(8,128)(2,1)S(1)}, bf16[128,640]{1,0:T(8,128)(2,1)S(1)}, u32[]{:S(2)}, u32[]{:S(2)}) collective-permute-start(bf16[128,640]{1,0:T(8,128)(2,1)S(1)} %get-tuple-element.42), channel_id=1, source_target_pairs={{0,5},{1,4},{4,1},{5,0},{8,13},{9,12},{12,9},{13,8},{2,7},{3,6},{6... | collective-permute-start | bytes 491528 | tf_op jit(solution)/shard_map/ppermute | solution.py:36
  110.3 12.6 %collective-permute-start.13 = (bf16[128,640]{1,0:T(8,128)(2,1)S(1)}, bf16[128,640]{1,0:T(8,128)(2,1)S(1)}, u32[]{:S(2)}, u32[]{:S(2)}) collective-permute-start(bf16[128,640]{1,0:T(8,128)(2,1)S(1)} %get-tuple-element.42), channel_id=1, source_target_pairs={{0,1},{1,0},{4,5},{5,4},{8,9},{9,8},{12,13},{13,12},{2,3},{3,2},{6... | collective-permute-start | bytes 491528 | tf_op jit(solution)/shard_map/ppermute | solution.py:36
  125.1 46.8 %all-to-all-start.2 = ((bf16[16,40,1280]{2,1,0:T(8,128)(2,1)}), bf16[16,40,1280]{2,1,0:T(8,128)(2,1)S(1)}, u32[]{:S(2)}, u32[]{:S(2)}) async-start(bf16[16,40,1280]{2,1,0:T(8,128)(2,1)} %bitcast.42), calls=%async_computation.2 | async-start | bytes 3276800 | tf_op jit(solution)/shard_map/all_to_all | solution.py:28
  131.1 32.7 %collective-permute-start.10 = (bf16[2,96,1280]{2,1,0:T(8,128)(2,1)S(1)}, bf16[2,96,1280]{2,1,0:T(8,128)(2,1)S(1)}, u32[]{:S(2)}, u32[]{:S(2)}) collective-permute-start(bf16[2,96,1280]{2,1,0:T(8,128)(2,1)S(1)} %copy-done.12), channel_id=1, source_target_pairs={{1,0},{2,1},{3,2},{4,3},{5,4},{6,5},{7,6},{8,7},{9,8},{10,9},{11,1... | collective-permute-start | bytes 1474568 | tf_op jit(solution)/shard_map/ppermute | solution.py:24
  134.0 29.8 %copy-start.7 = (bf16[2,128,1280]{2,1,0:T(8,128)(2,1)S(1)}, bf16[2,128,1280]{2,1,0:T(8,128)(2,1)}, u32[]{:S(2)}) copy-start(bf16[2,128,1280]{2,1,0:T(8,128)(2,1)} %get-tuple-element.17) | copy-start | bytes 1966084
  164.8 26.7 %collective-permute-start.11 = (bf16[2,128,1280]{2,1,0:T(8,128)(2,1)}, bf16[2,128,1280]{2,1,0:T(8,128)(2,1)}, u32[]{:S(2)}, u32[]{:S(2)}) collective-permute-start(bf16[2,128,1280]{2,1,0:T(8,128)(2,1)} %add_convert_fusion.2), channel_id=1, source_target_pairs={{16,0},{32,16},{48,32},{64,48},{80,64},{96,80},{112,96},{128,112},... | collective-permute-start | bytes 1966088 | tf_op jit(solution)/shard_map/ppermute | solution.py:24
  167.0 24.5 %collective-permute-start.12 = (bf16[2,128,1280]{2,1,0:T(8,128)(2,1)}, bf16[2,128,1280]{2,1,0:T(8,128)(2,1)}, u32[]{:S(2)}, u32[]{:S(2)}) collective-permute-start(bf16[2,128,1280]{2,1,0:T(8,128)(2,1)} %add_convert_fusion.1), channel_id=1, source_target_pairs={{0,16},{16,32},{32,48},{48,64},{64,80},{80,96},{96,112},{112,128},... | collective-permute-start | bytes 1966088 | tf_op jit(solution)/shard_map/ppermute | solution.py:24
  172.1 19.4 %copy-start.5 = (bf16[2,128,1280]{2,1,0:T(8,128)(2,1)S(1)}, bf16[2,128,1280]{2,1,0:T(8,128)(2,1)}, u32[]{:S(2)}) copy-start(bf16[2,128,1280]{2,1,0:T(8,128)(2,1)} %get-tuple-element.14) | copy-start | bytes 1966084
  (9 other events, 63.5 us)
where the time goes:
time: 195 us; the launch traced here: 194 us
  waiting for transfers between devices  73.3 us (38%)
  starting transfers between devices  58 us (30%)
  blocking collectives  18.5 us (9%)
  Pallas kernels  15.8 us (8%)
  other arithmetic  10.5 us (5%)
  matrix products  8.62 us (4%)
  local copies, waits for them, and re-layouts  8.01 us (4%)
    ppermute x8, waiting for transfers between devices, shifted(): lax.ppermute(value, axis, [(source, source + steps) for source in range(f...  43.8 us
    ppermute x8, starting transfers between devices, shifted(): lax.ppermute(value, axis, [(source, source + steps) for source in range(f...  24.9 us
    ppermute x8, waiting for transfers between devices, flipped(): return lax.ppermute(value, ('y', 'c'), pairs)  22.3 us
    all_to_all x3, starting transfers between devices, exchanged(): return lax.all_to_all(blocks, axis, 0, 0, tiled=True)  20.5 us
    all_to_all x1, blocking collectives, exchanged(): return lax.all_to_all(blocks, axis, 0, 0, tiled=True)  18.5 us
    ppermute x8, starting transfers between devices, flipped(): return lax.ppermute(value, ('y', 'c'), pairs)  12.6 us
    dot_general x4, matrix products, dot(): lax.dot_general(a, b, (((a_dim,), (b_dim,)), ((), ())), preferred_element...  8.62 us
    pallas_call x1, Pallas kernels, attention_grads(): pl.pallas_call(grads_kernel, grid=(inner // LANES // PER_STEP,), in_specs...  8.39 us
  transfers between devices with their start and end apart: 19, of which 8 were waited for; matrix products, arithmetic and copies ran while one was open for 9% of the time, Pallas kernels for 4%

commit v1 on v0

--- a/solution.py
+++ b/solution.py
@@ -68,40 +68,34 @@
     return (number * own_rows + row).reshape(-1)
 
 
-def key_places(row_count, col_count):
-    centre = (3, row_count, col_count)
-    edges = (2, 3, col_count)
-
-    def joined(first, second):
-        return jnp.concatenate([first.reshape(-1), second.reshape(-1)])
-
-    iota = lax.broadcasted_iota
-    frame = joined(iota(jnp.int32, centre, 0), iota(jnp.int32, edges, 1)) - 1
-    edge_row = iota(jnp.int32, edges, 0) * (row_count + 1) - 1
-    row = joined(iota(jnp.int32, centre, 1), edge_row)
-    tile = joined(iota(jnp.int32, centre, 2), iota(jnp.int32, edges, 2)) // TILE_W
-    return frame, row, tile
-
-
-def visible_keys(windows, frames_in_all, rows_in_all, row_count, col_count):
+def visible_groups(windows, frames_in_all, rows_in_all, row_count, col_count):
     time_index = lax.axis_index(TA)
     first_row = lax.axis_index(HA) * row_count
     tokens = row_count * col_count
     extent = jnp.repeat(windows[0], TILE_W, axis=1).reshape(tokens, 3)
-    frame, row, tile = key_places(row_count, col_count)
-    query = lax.broadcasted_iota(jnp.int32, (1, tokens), 1)
+    tiles = col_count // TILE_W
+    group = lax.broadcasted_iota(jnp.int32, (tokens, LANES), 1)
+    query = lax.broadcasted_iota(jnp.int32, (tokens, LANES), 0)
+    frame = group // ((row_count + 2) * tiles) - 1
+    row = group // tiles % (row_count + 2) - 1
+    tile = group % tiles
     inside = (
         (frame + time_index >= 0)
         & (frame + time_index < frames_in_all)
         & (row + first_row >= 0)
         & (row + first_row < rows_in_all)
-    )[:, None]
-    query_row = query // col_count
-    query_tile = query % col_count // TILE_W
-    inside = inside & (jnp.abs(frame)[:, None] <= extent[None, :, 0])
-    inside = inside & (jnp.abs(row[:, None] - query_row) <= extent[None, :, 1])
-    inside = inside & (jnp.abs(tile[:, None] - query_tile) <= extent[None, :, 2])
-    return jnp.where(inside, 0.0, NEG).astype(jnp.float32)
+        & (jnp.abs(frame) <= extent[:, 0:1])
+        & (jnp.abs(row - query // col_count) <= extent[:, 1:2])
+        & (jnp.abs(tile - query % col_count // TILE_W) <= extent[:, 2:3])
+    )
+    return jnp.where(inside, 0.0, NEG).astype(jnp.bfloat16)
+
+
+def key_groups(row_count, col_count):
+    keys = 3 * (row_count + 2) * col_count
+    key = lax.broadcasted_iota(jnp.int32, (keys, LANES), 0)
+    group = lax.broadcasted_iota(jnp.int32, (keys, LANES), 1)
+    return (key // TILE_W == group).astype(jnp.bfloat16)
 
 
 def stacked(pair):
@@ -132,15 +126,20 @@
     return stacked(q_ref[:, lanes] * jnp.asarray(HEAD_DIM**-0.5, jnp.bfloat16))
 
 
+def masked_scores(keys, groups_ref, queries, seen_ref):
+    seen = seen_ref[...]
+    wide_keys = jnp.concatenate([keys, groups_ref[...]], axis=1)
+    wide_queries = jnp.concatenate([queries, jnp.concatenate([seen, seen], axis=0)], axis=1)
+    return dot(wide_keys, wide_queries, 1, 1)
+
+
 def attend_kernel(q_ref, *refs):
-    near_refs = refs[:5]
-    bias_ref, out_ref, total_ref = refs[5:]
+    near_refs = refs[:3]
+    groups_ref, seen_ref, out_ref, total_ref = refs[3:]
     for i in range(PER_STEP):
         lanes = slice(i * LANES, (i + 1) * LANES)
         queries = scaled_queries(q_ref, lanes)
-        scores = dot(near(near_refs, 0, lanes), queries, 1, 1)
-        bias = bias_ref[...]
-        scores = scores + jnp.concatenate([bias, bias], axis=1)
+        scores = masked_scores(near(near_refs, 0, lanes), groups_ref, queries, seen_ref)
         top = jnp.max(scores, axis=0, keepdims=True)
         raised = jnp.exp(scores - top)
         total = jnp.sum(raised, axis=0, keepdims=True)
@@ -150,16 +149,15 @@
 
 
 def grads_kernel(q_ref, g_ref, total_ref, *refs):
-    near_refs = refs[:5]
-    bias_ref, dq_ref = refs[5:7]
-    out_refs = refs[7:]
+    near_refs = refs[:3]
+    groups_ref, seen_ref, dq_ref = refs[3:6]
+    out_refs = refs[6:]
     for i in range(PER_STEP):
         lanes = slice(i * LANES, (i + 1) * LANES)
         queries = scaled_queries(q_ref, lanes)
         grads = stacked(g_ref[:, lanes])
         keys = near(near_refs, 0, lanes)
-        bias = bias_ref[...]
-        scores = dot(keys, queries, 1, 1) + jnp.concatenate([bias, bias], axis=1)
+        scores = masked_scores(keys, groups_ref, queries, seen_ref)
         weights = jnp.exp(scores - total_ref[i, 0:1, :])
         dweights = weights * dot(near(near_refs, 1, lanes), grads, 1, 1)
         delta = jnp.sum(dweights, axis=0, keepdims=True)
@@ -176,22 +174,22 @@
             first = last
 
 
-def specs(tokens, nearby, bias):
+def specs(tokens, nearby, mask):
     width = PER_STEP * LANES
     by_pair = pl.BlockSpec((tokens, width), lambda j: (0, j))
     near_specs = [pl.BlockSpec((*x.shape[:2], width), lambda j: (0, 0, j)) for x in nearby]
     totals = pl.BlockSpec((PER_STEP, 8, 2 * tokens), lambda j: (j, 0, 0))
-    return by_pair, near_specs, totals, pl.BlockSpec(bias.shape, lambda j: (0, 0))
-
-
-def attend(queries, nearby, bias):
+    return by_pair, near_specs, totals, [pl.BlockSpec(x.shape, lambda j: (0, 0)) for x in mask]
+
+
+def attend(queries, nearby, mask):
     tokens, inner = queries.shape
-    keys = bias.shape[0]
-    by_pair, near_specs, totals, bias_spec = specs(tokens, nearby, bias)
+    keys = mask[0].shape[0]
+    by_pair, near_specs, totals, mask_specs = specs(tokens, nearby, mask)
     return pl.pallas_call(
         attend_kernel,
         grid=(inner // LANES // PER_STEP,),
-        in_specs=[by_pair, *near_specs, bias_spec],
+        in_specs=[by_pair, *near_specs, *mask_specs],
         out_specs=[by_pair, totals],
         out_shape=[
             jax.ShapeDtypeStruct((tokens, inner), jnp.bfloat16),
@@ -201,17 +199,17 @@
             flops=8 * keys * tokens * inner, bytes_accessed=4 * keys * inner,
             transcendentals=keys * tokens * 20),
         name="attend",
-    )(queries, *nearby, bias)
-
-
-def attention_grads(queries, grads, totals, nearby, bias):
+    )(queries, *nearby, *mask)
+
+
+def attention_grads(queries, grads, totals, nearby, mask):
     tokens, inner = queries.shape
-    keys = bias.shape[0]
-    by_pair, near_specs, totals_spec, bias_spec = specs(tokens, nearby, bias)
+    keys = mask[0].shape[0]
+    by_pair, near_specs, totals_spec, mask_specs = specs(tokens, nearby, mask)
     return pl.pallas_call(
         grads_kernel,
         grid=(inner // LANES // PER_STEP,),
-        in_specs=[by_pair, by_pair, totals_spec, *near_specs, bias_spec],
+        in_specs=[by_pair, by_pair, totals_spec, *near_specs, *mask_specs],
         out_specs=[by_pair, *near_specs],
         out_shape=[jax.ShapeDtypeStruct((tokens, inner), jnp.bfloat16)]
         + [jax.ShapeDtypeStruct(x.shape, jnp.bfloat16) for x in nearby],
@@ -219,7 +217,7 @@
             flops=20 * keys * tokens * inner, bytes_accessed=8 * keys * inner,
             transcendentals=keys * tokens * 20),
         name="attention_grads",
-    )(queries, grads, totals, *nearby, bias)
+    )(queries, grads, totals, *nearby, *mask)
 
 
 def step(queries, keys, values, grad_out, out_weight, windows):
@@ -233,10 +231,10 @@
     flat_grad = grad_out.reshape(tokens, model_width)
 
     own = jnp.stack([keys.reshape(tokens, inner), values.reshape(tokens, inner)])
-    centre = (shifted(own, TA, 1), own, shifted(own, TA, -1))
-    top = jnp.concatenate([x[:, :col_count] for x in centre], axis=1)
-    bottom = jnp.concatenate([x[:, tokens - col_count :] for x in centre], axis=1)
-    nearby = (*centre, shifted(bottom, HA, 1), shifted(top, HA, -1))
+    below = shifted(own[:, tokens - col_count :], HA, 1)
+    above = shifted(own[:, :col_count], HA, -1)
+    wide = jnp.concatenate([below, own, above], axis=1)
+    nearby = (shifted(wide, TA, 1), wide, shifted(wide, TA, -1))
 
     wide_half = model_width // 2
     odd = lax.axis_index("y") % 2
@@ -251,9 +249,12 @@
     weight = gathered_weight(out_weight)
     order = row_order(out_weight.shape[0])
     picks = (order[:, None] == lax.broadcasted_iota(jnp.int32, (1, inner), 1)).astype(jnp.bfloat16)
-    bias = visible_keys(windows, all_frames, all_rows, row_count, col_count)
-
-    attended, totals = attend(flat_queries, nearby, bias)
+    mask = (
+        key_groups(row_count, col_count),
+        visible_groups(windows, all_frames, all_rows, row_count, col_count),
+    )
+
+    attended, totals = attend(flat_queries, nearby, mask)
     picked = dot(attended, picks, 1, 1).astype(jnp.bfloat16)
     half = inner // 2
     group_attended = jnp.concatenate(
@@ -274,21 +275,17 @@
     split_attn = jnp.concatenate([own_half, other_half], axis=1).astype(jnp.bfloat16)
     grad_attn = dot(split_attn, picks, 1, 0).astype(jnp.bfloat16)
 
-    query_grad, *pieces = attention_grads(flat_queries, grad_attn, totals, nearby, bias)
-    to_bottom = shifted(pieces[3], HA, -1).astype(jnp.float32)
-    to_top = shifted(pieces[4], HA, 1).astype(jnp.float32)
-    rest = jnp.zeros_like(pieces[0][:, : tokens - col_count], jnp.float32)
-
-    def with_edges(i):
-        at = slice(i * col_count, (i + 1) * col_count)
-        return (pieces[i].astype(jnp.float32)
-                + jnp.concatenate([to_top[:, at], rest], axis=1)
-                + jnp.concatenate([rest, to_bottom[:, at]], axis=1))
-
-    before, here, after = [with_edges(i) for i in range(3)]
-    before = shifted(before.astype(jnp.bfloat16), TA, -1)
-    after = shifted(after.astype(jnp.bfloat16), TA, 1)
-    total = (here + before.astype(jnp.float32) + after.astype(jnp.float32)).astype(jnp.bfloat16)
+    query_grad, before, here, after = attention_grads(flat_queries, grad_attn, totals, nearby, mask)
+    before = shifted(before, TA, -1)
+    after = shifted(after, TA, 1)
+    here = here.astype(jnp.float32) + before.astype(jnp.float32) + after.astype(jnp.float32)
+    low = here[:, :col_count].astype(jnp.bfloat16)
+    high = here[:, tokens + col_count :].astype(jnp.bfloat16)
+    low = shifted(low, HA, -1).astype(jnp.float32)
+    high = shifted(high, HA, 1).astype(jnp.float32)
+    rest = jnp.zeros_like(here[:, : tokens - col_count])
+    total = (here[:, col_count : tokens + col_count] + jnp.concatenate([high, rest], axis=1)
+             + jnp.concatenate([rest, low], axis=1)).astype(jnp.bfloat16)
     return (
         query_grad.reshape(queries.shape),
         total[0].reshape(queries.shape),

time: 195 us -> 177 us (0.908)
  the two profiles are of different devices: /device:TPU:25 before, /device:TPU:15 now
where the time goes in v1:
time: 177 us
  waiting for transfers between devices  75.7 us (43%)
  starting transfers between devices  62.1 us (35%)
  Pallas kernels  14.9 us (8%)
  matrix products  9.69 us (5%)
  other arithmetic  8.01 us (5%)
  local copies, waits for them, and re-layouts  5.07 us (3%)
    ppermute x8, waiting for transfers between devices, shifted(): lax.ppermute(value, axis, [(source, source + steps) for source in range(f...  48.2 us
    all_to_all x4, starting transfers between devices, exchanged(): return lax.all_to_all(blocks, axis, 0, 0, tiled=True)  28.7 us
    ppermute x8, starting transfers between devices, shifted(): lax.ppermute(value, axis, [(source, source + steps) for source in range(f...  28.5 us
    ppermute x8, waiting for transfers between devices, flipped(): return lax.ppermute(value, ('y', 'c'), pairs)  27.5 us
    dot_general x4, matrix products, dot(): lax.dot_general(a, b, (((a_dim,), (b_dim,)), ((), ())), preferred_element...  9.69 us
    pallas_call x1, Pallas kernels, attention_grads(): pl.pallas_call(grads_kernel, grid=(inner // LANES // PER_STEP,), in_specs...  8.27 us
    pallas_call x1, Pallas kernels, attend(): pl.pallas_call(attend_kernel, grid=(inner // LANES // PER_STEP,), in_spec...  6.6 us
    ppermute x8, starting transfers between devices, flipped(): return lax.ppermute(value, ('y', 'c'), pairs)  4.92 us
  transfers between devices with their start and end apart: 20, of which 9 were waited for; matrix products, arithmetic and copies ran while one was open for 11% of the time, Pallas kernels for 8%

profile of v1, /device:TPU:15, one launch (start us, length us, event | category | flops | bytes accessed | tf_op | source)
XLA Modules:
  0.0 176.6 jit_solution(11592080730199874904)
XLA Ops:
  2.2 8.3 %all-to-all-start = ((bf16[8,5,2560]{2,1,0:T(8,128)(2,1)}), bf16[8,5,2560]{2,1,0:T(8,128)(2,1)S(1)}, u32[]{:S(2)}, u32[]{:S(2)}) async-start(bf16[8,5,2560]{2,1,0:T(8,128)(2,1)} %broadcast_in_dim.24), calls=%async_computation | async-start | bytes 655360 | tf_op jit(solution)/shard_map/all_to_all | solution.py:28
  11.6 4.3 %collective-permute-start.5 = (bf16[2,32,1280]{2,1,0:T(8,128)(2,1)S(1)}, bf16[2,32,1280]{2,1,0:T(8,128)(2,1)S(1)}, u32[]{:S(2)}, u32[]{:S(2)}) collective-permute-start(bf16[2,32,1280]{2,1,0:T(8,128)(2,1)S(1)} %get-tuple-element.22), channel_id=1, source_target_pairs={{0,1},{1,2},{2,3},{3,4},{4,5},{5,6},{6,7},{7,8},{8,9},{9,10},{10,1... | collective-permute-start | bytes 491528 | tf_op jit(solution)/shard_map/ppermute | solution.py:24
  19.5 4.2 %collective-permute-done.6 = bf16[2,32,1280]{2,1,0:T(8,128)(2,1)S(1)} collective-permute-done((bf16[2,32,1280]{2,1,0:T(8,128)(2,1)S(1)}, bf16[2,32,1280]{2,1,0:T(8,128)(2,1)S(1)}, u32[]{:S(2)}, u32[]{:S(2)}) %collective-permute-start.6) | collective-permute-done | bytes 163872 | tf_op jit(solution)/shard_map/ppermute | solution.py:24
  23.8 5.1 %collective-permute-start.8 = (bf16[2,192,1280]{2,1,0:T(8,128)(2,1)S(1)}, bf16[2,192,1280]{2,1,0:T(8,128)(2,1)}, u32[]{:S(2)}, u32[]{:S(2)}) collective-permute-start(bf16[2,192,1280]{2,1,0:T(8,128)(2,1)S(1)} %pad_maximum_fusion.1.refs_1_), channel_id=1, source_target_pairs={{16,0},{32,16},{48,32},{64,48},{80,64},{96,80},{112,96},{128,112},... | collective-permute-start | bytes 2949128 | tf_op jit(solution)/shard_map/ppermute | solution.py:24
  29.0 1.9 %collective-permute-start.7 = (bf16[2,192,1280]{2,1,0:T(8,128)(2,1)S(1)}, bf16[2,192,1280]{2,1,0:T(8,128)(2,1)}, u32[]{:S(2)}, u32[]{:S(2)}) collective-permute-start(bf16[2,192,1280]{2,1,0:T(8,128)(2,1)S(1)} %pad_maximum_fusion.1.refs_1_), channel_id=1, source_target_pairs={{0,16},{16,32},{32,48},{48,64},{64,80},{80,96},{96,112},{112,128},... | collective-permute-start | bytes 2949128 | tf_op jit(solution)/shard_map/ppermute | solution.py:24
  34.1 6.3 %all-to-all-start.1 = ((bf16[16,40,1280]{2,1,0:T(8,128)(2,1)}), bf16[16,40,1280]{2,1,0:T(8,128)(2,1)}, u32[]{:S(2)}, u32[]{:S(2)}) async-start(bf16[16,40,1280]{2,1,0:T(8,128)(2,1)} %bitcast.9), calls=%async_computation.1 | async-start | bytes 3276800 | tf_op jit(solution)/shard_map/all_to_all | solution.py:28
  41.5 7.3 %collective-permute-done.8.refs_2_ = bf16[2,192,1280]{2,1,0:T(8,128)(2,1)} collective-permute-done((bf16[2,192,1280]{2,1,0:T(8,128)(2,1)S(1)}, bf16[2,192,1280]{2,1,0:T(8,128)(2,1)}, u32[]{:S(2)}, u32[]{:S(2)}) %collective-permute-start.8) | collective-permute-done | bytes 983072 | tf_op jit(solution)/shard_map/ppermute | solution.py:24
  48.8 8.0 %collective-permute-done.7.refs_0_ = bf16[2,192,1280]{2,1,0:T(8,128)(2,1)} collective-permute-done((bf16[2,192,1280]{2,1,0:T(8,128)(2,1)S(1)}, bf16[2,192,1280]{2,1,0:T(8,128)(2,1)}, u32[]{:S(2)}, u32[]{:S(2)}) %collective-permute-start.7) | collective-permute-done | bytes 983072 | tf_op jit(solution)/shard_map/ppermute | solution.py:24
  56.8 6.6 %attend.1 = (bf16[128,1280]{1,0:T(8,128)(2,1)}, f32[10,8,256]{2,1,0:T(8,128)}) custom-call(bf16[128,1280]{1,0:T(8,128)(2,1)} %bitcast.52, bf16[2,192,1280]{2,1,0:T(8,128)(2,1)} %collective-permute-done.7.refs_0_, bf16[2,192,1280]{2,1,0:T(8,128)(2,1)} %copy-done, bf16[2,192,1280]{2,1,0:T(8,128)(2,1)} %collective-permute-done.8.refs_2_, ...), custom_call_target="tpu_custom_call" | custom-call | flops 754974720 | bytes 2949120 | tf_op jit(solution)/shard_map/attend/pallas_call | solution.py:189
  63.4 2.5 %fusion.6 = bf16[128,1280]{1,0:T(8,128)(2,1)S(1)} fusion(bf16[128,1280]{1,0:T(8,128)(2,1)} %get-tuple-element.15, s32[1280]{0:T(1024)S(1)} %fusion.48), kind=kOutput, calls=%fused_computation.8 | convolution fusion | flops 421232640 | bytes 660480 | tf_op jit(solution)/shard_map/dot_general | solution.py:116
  68.0 7.8 %collective-permute-done.14 = bf16[128,640]{1,0:T(8,128)(2,1)S(1)} collective-permute-done((bf16[128,640]{1,0:T(8,128)(2,1)S(1)}, bf16[128,640]{1,0:T(8,128)(2,1)S(1)}, u32[]{:S(2)}, u32[]{:S(2)}) %collective-permute-start.14) | collective-permute-done | bytes 163872 | tf_op jit(solution)/shard_map/ppermute | solution.py:36
  75.9 2.2 %fusion.4 = bf16[640,1280]{1,0:T(8,128)(2,1)} fusion(bf16[512,1280]{1,0:T(8,128)(2,1)S(1)} %bitcast.41, bf16[128,640]{1,0:T(8,128)(2,1)S(1)} %collective-permute-done.15, bf16[128,640]{1,0:T(8,128)(2,1)S(1)} %collective-permute-done.14, bf16[128,640]{1,0:T(8,128)(2,1)S(1)} %collective-permute-done.13, bf16[128,640]{1,0:T(8,128)(2,1)S(1)} %get-tuple-element.31), kind=kOutput, calls=%fused_computation.6 | convolution fusion | flops 843120640 | bytes 3604480 | tf_op jit(solution)/shard_map/dot_general | solution.py:116
  78.1 10.7 %all-to-all-start.2 = ((bf16[16,40,1280]{2,1,0:T(8,128)(2,1)}), bf16[16,40,1280]{2,1,0:T(8,128)(2,1)S(1)}, u32[]{:S(2)}, u32[]{:S(2)}) async-start(bf16[16,40,1280]{2,1,0:T(8,128)(2,1)} %bitcast.20), calls=%async_computation.2 | async-start | bytes 3276800 | tf_op jit(solution)/shard_map/all_to_all | solution.py:28
  88.8 2.6 %fusion.62 = (bf16[512,640]{1,0:T(8,128)(2,1)S(1)}, f32[512,640]{1,0:T(8,128)S(1)}) fusion(bf16[512,1280]{1,0:T(8,128)(2,1)S(1)} %bitcast.42, bf16[640,1280]{1,0:T(8,128)(2,1)} %bitcast.10), kind=kOutput, calls=%fused_computation.128 | convolution fusion | flops 839188480 | bytes 4915200 | tf_op jit(solution)/shard_map/dot_general | solution.py:116
  94.1 18.4 %collective-permute-done.4 = bf16[128,640]{1,0:T(8,128)(2,1)S(1)} collective-permute-done((bf16[128,640]{1,0:T(8,128)(2,1)S(1)}, bf16[128,640]{1,0:T(8,128)(2,1)S(1)}, u32[]{:S(2)}, u32[]{:S(2)}) %collective-permute-start.4) | collective-permute-done | bytes 163872 | tf_op jit(solution)/shard_map/ppermute | solution.py:36
  113.9 2.3 %fusion.5.g_ref = bf16[128,1280]{1,0:T(8,128)(2,1)} fusion(s32[1280]{0:T(1024)S(1)} %fusion.48, bf16[128,640]{1,0:T(8,128)(2,1)S(1)} %add_convert_fusion, bf16[128,640]{1,0:T(8,128)(2,1)S(1)} %fusion.16), kind=kOutput, calls=%fused_computation.7 | convolution fusion | flops 421888000 | bytes 660480 | tf_op jit(solution)/shard_map/dot_general | solution.py:116
  116.1 8.3 %attention_grads.1 = (bf16[128,1280]{1,0:T(8,128)(2,1)}, bf16[2,192,1280]{2,1,0:T(8,128)(2,1)}, bf16[2,192,1280]{2,1,0:T(8,128)(2,1)}, bf16[2,192,1280]{2,1,0:T(8,128)(2,1)}) custom-call(bf16[128,1280]{1,0:T(8,128)(2,1)} %bitcast.53, bf16[128,1280]{1,0:T(8,128)(2,1)} %fusion.5.g_ref, f32[10,8,256]{2,1,0:T(8,128)} %get-tuple-element.10.total_ref, ...), custom_call_target="tpu_custom_call" | custom-call | flops 1887436800 | bytes 5898240 | tf_op jit(solution)/shard_map/attention_grads/pallas_call | solution.py:209
  126.3 3.4 %collective-permute-start.10 = (bf16[2,192,1280]{2,1,0:T(8,128)(2,1)}, bf16[2,192,1280]{2,1,0:T(8,128)(2,1)}, u32[]{:S(2)}, u32[]{:S(2)}) collective-permute-start(bf16[2,192,1280]{2,1,0:T(8,128)(2,1)} %get-tuple-element.14), channel_id=1, source_target_pairs={{0,16},{16,32},{32,48},{48,64},{64,80},{80,96},{96,112},{112,128},... | collective-permute-start | bytes 2949128 | tf_op jit(solution)/shard_map/ppermute | solution.py:24
  130.9 3.4 %all-to-all-start.3 = ((bf16[8,5,2560]{2,1,0:T(8,128)(2,1)}), bf16[8,5,2560]{2,1,0:T(8,128)(2,1)S(1)}, u32[]{:S(2)}, u32[]{:S(2)}) async-start(bf16[8,5,2560]{2,1,0:T(8,128)(2,1)} %pad_maximum_fusion.3), calls=%async_computation.3 | async-start | bytes 655360 | tf_op jit(solution)/shard_map/all_to_all | solution.py:28
  134.3 17.4 %collective-permute-done.9 = bf16[2,192,1280]{2,1,0:T(8,128)(2,1)} collective-permute-done((bf16[2,192,1280]{2,1,0:T(8,128)(2,1)}, bf16[2,192,1280]{2,1,0:T(8,128)(2,1)}, u32[]{:S(2)}, u32[]{:S(2)}) %collective-permute-start.9) | collective-permute-done | bytes 983072 | tf_op jit(solution)/shard_map/ppermute | solution.py:24
  151.8 6.4 %collective-permute-done.10 = bf16[2,192,1280]{2,1,0:T(8,128)(2,1)} collective-permute-done((bf16[2,192,1280]{2,1,0:T(8,128)(2,1)}, bf16[2,192,1280]{2,1,0:T(8,128)(2,1)}, u32[]{:S(2)}, u32[]{:S(2)}) %collective-permute-start.10) | collective-permute-done | bytes 983072 | tf_op jit(solution)/shard_map/ppermute | solution.py:24
  160.1 8.0 %collective-permute-start.11 = (bf16[2,32,1280]{2,1,0:T(8,128)(2,1)S(1)}, bf16[2,32,1280]{2,1,0:T(8,128)(2,1)S(1)}, u32[]{:S(2)}, u32[]{:S(2)}) collective-permute-start(bf16[2,32,1280]{2,1,0:T(8,128)(2,1)S(1)} %get-tuple-element.18), channel_id=1, source_target_pairs={{0,1},{1,2},{2,3},{3,4},{4,5},{5,6},{6,7},{7,8},{8,9},{9,10},{10,1... | collective-permute-start | bytes 491528 | tf_op jit(solution)/shard_map/ppermute | solution.py:24
  168.1 1.9 %collective-permute-start.12 = (bf16[2,32,1280]{2,1,0:T(8,128)(2,1)S(1)}, bf16[2,32,1280]{2,1,0:T(8,128)(2,1)S(1)}, u32[]{:S(2)}, u32[]{:S(2)}) collective-permute-start(bf16[2,32,1280]{2,1,0:T(8,128)(2,1)S(1)} %get-tuple-element.19), channel_id=1, source_target_pairs={{1,0},{2,1},{3,2},{4,3},{5,4},{6,5},{7,6},{8,7},{9,8},{10,9},{11,1... | collective-permute-start | bytes 491528 | tf_op jit(solution)/shard_map/ppermute | solution.py:24
  170.7 4.9 %collective-permute-done.12 = bf16[2,32,1280]{2,1,0:T(8,128)(2,1)S(1)} collective-permute-done((bf16[2,32,1280]{2,1,0:T(8,128)(2,1)S(1)}, bf16[2,32,1280]{2,1,0:T(8,128)(2,1)S(1)}, u32[]{:S(2)}, u32[]{:S(2)}) %collective-permute-start.12) | collective-permute-done | bytes 163872 | tf_op jit(solution)/shard_map/ppermute | solution.py:24
  (84 shorter events, 23.1 us)
Async XLA Ops:
  0.6 17.7 %copy-start.5 = (s32[1,4,4,3]{2,1,3,0:T(4,128)S(1)}, s32[1,4,4,3]{2,1,3,0:T(4,128)}, u32[]{:S(2)}) copy-start(s32[1,4,4,3]{2,1,3,0:T(4,128)} %param.11) | copy-start | bytes 580
  2.2 21.5 %copy-start.1 = (bf16[1,4,32,1280]{3,2,1,0:T(8,128)(2,1)S(1)}, bf16[1,4,32,1280]{3,2,1,0:T(8,128)(2,1)}, u32[]{:S(2)}) copy-start(bf16[1,4,32,1280]{3,2,1,0:T(8,128)(2,1)} %param.8) | copy-start | bytes 983044
  2.2 21.5 %copy-start.2 = (bf16[1,4,32,1280]{3,2,1,0:T(8,128)(2,1)S(1)}, bf16[1,4,32,1280]{3,2,1,0:T(8,128)(2,1)}, u32[]{:S(2)}) copy-start(bf16[1,4,32,1280]{3,2,1,0:T(8,128)(2,1)} %param.7) | copy-start | bytes 983044
  2.2 30.4 %all-to-all-start = ((bf16[8,5,2560]{2,1,0:T(8,128)(2,1)}), bf16[8,5,2560]{2,1,0:T(8,128)(2,1)S(1)}, u32[]{:S(2)}, u32[]{:S(2)}) async-start(bf16[8,5,2560]{2,1,0:T(8,128)(2,1)} %broadcast_in_dim.24), calls=%async_computation | async-start | bytes 655360 | tf_op jit(solution)/shard_map/all_to_all | solution.py:28
  11.6 7.9 %collective-permute-start.5 = (bf16[2,32,1280]{2,1,0:T(8,128)(2,1)S(1)}, bf16[2,32,1280]{2,1,0:T(8,128)(2,1)S(1)}, u32[]{:S(2)}, u32[]{:S(2)}) collective-permute-start(bf16[2,32,1280]{2,1,0:T(8,128)(2,1)S(1)} %get-tuple-element.22), channel_id=1, source_target_pairs={{0,1},{1,2},{2,3},{3,4},{4,5},{5,6},{6,7},{7,8},{8,9},{9,10},{10,1... | collective-permute-start | bytes 491528 | tf_op jit(solution)/shard_map/ppermute | solution.py:24
  15.9 7.8 %collective-permute-start.6 = (bf16[2,32,1280]{2,1,0:T(8,128)(2,1)S(1)}, bf16[2,32,1280]{2,1,0:T(8,128)(2,1)S(1)}, u32[]{:S(2)}, u32[]{:S(2)}) collective-permute-start(bf16[2,32,1280]{2,1,0:T(8,128)(2,1)S(1)} %get-tuple-element.23), channel_id=1, source_target_pairs={{1,0},{2,1},{3,2},{4,3},{5,4},{6,5},{7,6},{8,7},{9,8},{10,9},{11,1... | collective-permute-start | bytes 491528 | tf_op jit(solution)/shard_map/ppermute | solution.py:24
  17.9 22.4 %collective-permute-start = (bf16[128,1280]{1,0:T(8,128)(2,1)S(1)}, bf16[128,1280]{1,0:T(8,128)(2,1)}, u32[]{:S(2)}, u32[]{:S(2)}) collective-permute-start(bf16[128,1280]{1,0:T(8,128)(2,1)S(1)} %get-tuple-element.30), channel_id=1, source_target_pairs={{0,4},{1,5},{4,0},{5,1},{8,12},{9,13},{12,8},{13,9},{2,6},{3,7},{6... | collective-permute-start | bytes 983048 | tf_op jit(solution)/shard_map/ppermute | solution.py:36
  23.8 25.0 %collective-permute-start.8 = (bf16[2,192,1280]{2,1,0:T(8,128)(2,1)S(1)}, bf16[2,192,1280]{2,1,0:T(8,128)(2,1)}, u32[]{:S(2)}, u32[]{:S(2)}) collective-permute-start(bf16[2,192,1280]{2,1,0:T(8,128)(2,1)S(1)} %pad_maximum_fusion.1.refs_1_), channel_id=1, source_target_pairs={{16,0},{32,16},{48,32},{64,48},{80,64},{96,80},{112,96},{128,112},... | collective-permute-start | bytes 2949128 | tf_op jit(solution)/shard_map/ppermute | solution.py:24
  29.0 27.8 %collective-permute-start.7 = (bf16[2,192,1280]{2,1,0:T(8,128)(2,1)S(1)}, bf16[2,192,1280]{2,1,0:T(8,128)(2,1)}, u32[]{:S(2)}, u32[]{:S(2)}) collective-permute-start(bf16[2,192,1280]{2,1,0:T(8,128)(2,1)S(1)} %pad_maximum_fusion.1.refs_1_), channel_id=1, source_target_pairs={{0,16},{16,32},{32,48},{48,64},{64,80},{80,96},{96,112},{112,128},... | collective-permute-start | bytes 2949128 | tf_op jit(solution)/shard_map/ppermute | solution.py:24
  34.1 44.0 %all-to-all-start.1 = ((bf16[16,40,1280]{2,1,0:T(8,128)(2,1)}), bf16[16,40,1280]{2,1,0:T(8,128)(2,1)}, u32[]{:S(2)}, u32[]{:S(2)}) async-start(bf16[16,40,1280]{2,1,0:T(8,128)(2,1)} %bitcast.9), calls=%async_computation.1 | async-start | bytes 3276800 | tf_op jit(solution)/shard_map/all_to_all | solution.py:28
  41.4 26.5 %collective-permute-start.1 = (bf16[2,128,1280]{2,1,0:T(8,128)(2,1)S(1)}, bf16[2,128,1280]{2,1,0:T(8,128)(2,1)S(1)}, u32[]{:S(2)}, u32[]{:S(2)}) collective-permute-start(bf16[2,128,1280]{2,1,0:T(8,128)(2,1)S(1)} %get-tuple-element.28), channel_id=1, source_target_pairs={{0,1},{1,0},{4,5},{5,4},{8,9},{9,8},{12,13},{13,12},{2,3},{3,2},{6... | collective-permute-start | bytes 1966088 | tf_op jit(solution)/shard_map/ppermute | solution.py:36
  66.0 9.9 %collective-permute-start.15 = (bf16[128,640]{1,0:T(8,128)(2,1)S(1)}, bf16[128,640]{1,0:T(8,128)(2,1)S(1)}, u32[]{:S(2)}, u32[]{:S(2)}) collective-permute-start(bf16[128,640]{1,0:T(8,128)(2,1)S(1)} %get-tuple-element.32), channel_id=1, source_target_pairs={{0,5},{1,4},{4,1},{5,0},{8,13},{9,12},{12,9},{13,8},{2,7},{3,6},{6... | collective-permute-start | bytes 491528 | tf_op jit(solution)/shard_map/ppermute | solution.py:36
  66.1 9.8 %collective-permute-start.13 = (bf16[128,640]{1,0:T(8,128)(2,1)S(1)}, bf16[128,640]{1,0:T(8,128)(2,1)S(1)}, u32[]{:S(2)}, u32[]{:S(2)}) collective-permute-start(bf16[128,640]{1,0:T(8,128)(2,1)S(1)} %get-tuple-element.32), channel_id=1, source_target_pairs={{0,1},{1,0},{4,5},{5,4},{8,9},{9,8},{12,13},{13,12},{2,3},{3,2},{6... | collective-permute-start | bytes 491528 | tf_op jit(solution)/shard_map/ppermute | solution.py:36
  67.0 8.8 %collective-permute-start.14 = (bf16[128,640]{1,0:T(8,128)(2,1)S(1)}, bf16[128,640]{1,0:T(8,128)(2,1)S(1)}, u32[]{:S(2)}, u32[]{:S(2)}) collective-permute-start(bf16[128,640]{1,0:T(8,128)(2,1)S(1)} %get-tuple-element.31), channel_id=1, source_target_pairs={{0,4},{1,5},{4,0},{5,1},{8,12},{9,13},{12,8},{13,9},{2,6},{3,7},{6... | collective-permute-start | bytes 491528 | tf_op jit(solution)/shard_map/ppermute | solution.py:36
  78.1 51.6 %all-to-all-start.2 = ((bf16[16,40,1280]{2,1,0:T(8,128)(2,1)}), bf16[16,40,1280]{2,1,0:T(8,128)(2,1)S(1)}, u32[]{:S(2)}, u32[]{:S(2)}) async-start(bf16[16,40,1280]{2,1,0:T(8,128)(2,1)} %bitcast.20), calls=%async_computation.2 | async-start | bytes 3276800 | tf_op jit(solution)/shard_map/all_to_all | solution.py:28
  91.5 21.1 %collective-permute-start.4 = (bf16[128,640]{1,0:T(8,128)(2,1)S(1)}, bf16[128,640]{1,0:T(8,128)(2,1)S(1)}, u32[]{:S(2)}, u32[]{:S(2)}) collective-permute-start(bf16[128,640]{1,0:T(8,128)(2,1)S(1)} %get-tuple-element.25), channel_id=1, source_target_pairs={{0,5},{1,4},{4,1},{5,0},{8,13},{9,12},{12,9},{13,8},{2,7},{3,6},{6... | collective-permute-start | bytes 491528 | tf_op jit(solution)/shard_map/ppermute | solution.py:36
  93.0 19.6 %collective-permute-start.3 = (bf16[128,640]{1,0:T(8,128)(2,1)S(1)}, bf16[128,640]{1,0:T(8,128)(2,1)S(1)}, u32[]{:S(2)}, u32[]{:S(2)}) collective-permute-start(bf16[128,640]{1,0:T(8,128)(2,1)S(1)} %get-tuple-element.26), channel_id=1, source_target_pairs={{0,1},{1,0},{4,5},{5,4},{8,9},{9,8},{12,13},{13,12},{2,3},{3,2},{6... | collective-permute-start | bytes 491528 | tf_op jit(solution)/shard_map/ppermute | solution.py:36
  93.0 20.9 %collective-permute-start.2 = (bf16[128,640]{1,0:T(8,128)(2,1)S(1)}, bf16[128,640]{1,0:T(8,128)(2,1)S(1)}, u32[]{:S(2)}, u32[]{:S(2)}) collective-permute-start(bf16[128,640]{1,0:T(8,128)(2,1)S(1)} %get-tuple-element.24), channel_id=1, source_target_pairs={{0,4},{1,5},{4,0},{5,1},{8,12},{9,13},{12,8},{13,9},{2,6},{3,7},{6... | collective-permute-start | bytes 491528 | tf_op jit(solution)/shard_map/ppermute | solution.py:36
  124.4 27.3 %collective-permute-start.9 = (bf16[2,192,1280]{2,1,0:T(8,128)(2,1)}, bf16[2,192,1280]{2,1,0:T(8,128)(2,1)}, u32[]{:S(2)}, u32[]{:S(2)}) collective-permute-start(bf16[2,192,1280]{2,1,0:T(8,128)(2,1)} %get-tuple-element.13), channel_id=1, source_target_pairs={{16,0},{32,16},{48,32},{64,48},{80,64},{96,80},{112,96},{128,112},... | collective-permute-start | bytes 2949128 | tf_op jit(solution)/shard_map/ppermute | solution.py:24
  126.3 31.8 %collective-permute-start.10 = (bf16[2,192,1280]{2,1,0:T(8,128)(2,1)}, bf16[2,192,1280]{2,1,0:T(8,128)(2,1)}, u32[]{:S(2)}, u32[]{:S(2)}) collective-permute-start(bf16[2,192,1280]{2,1,0:T(8,128)(2,1)} %get-tuple-element.14), channel_id=1, source_target_pairs={{0,16},{16,32},{32,48},{48,64},{64,80},{80,96},{96,112},{112,128},... | collective-permute-start | bytes 2949128 | tf_op jit(solution)/shard_map/ppermute | solution.py:24
  129.7 28.5 %copy-start.3 = (bf16[2,192,1280]{2,1,0:T(8,128)(2,1)S(1)}, bf16[2,192,1280]{2,1,0:T(8,128)(2,1)}, u32[]{:S(2)}) copy-start(bf16[2,192,1280]{2,1,0:T(8,128)(2,1)} %get-tuple-element.12) | copy-start | bytes 2949124
  130.9 39.1 %all-to-all-start.3 = ((bf16[8,5,2560]{2,1,0:T(8,128)(2,1)}), bf16[8,5,2560]{2,1,0:T(8,128)(2,1)S(1)}, u32[]{:S(2)}, u32[]{:S(2)}) async-start(bf16[8,5,2560]{2,1,0:T(8,128)(2,1)} %pad_maximum_fusion.3), calls=%async_computation.3 | async-start | bytes 655360 | tf_op jit(solution)/shard_map/all_to_all | solution.py:28
  160.1 10.6 %collective-permute-start.11 = (bf16[2,32,1280]{2,1,0:T(8,128)(2,1)S(1)}, bf16[2,32,1280]{2,1,0:T(8,128)(2,1)S(1)}, u32[]{:S(2)}, u32[]{:S(2)}) collective-permute-start(bf16[2,32,1280]{2,1,0:T(8,128)(2,1)S(1)} %get-tuple-element.18), channel_id=1, source_target_pairs={{0,1},{1,2},{2,3},{3,4},{4,5},{5,6},{6,7},{7,8},{8,9},{9,10},{10,1... | collective-permute-start | bytes 491528 | tf_op jit(solution)/shard_map/ppermute | solution.py:24
  168.1 7.5 %collective-permute-start.12 = (bf16[2,32,1280]{2,1,0:T(8,128)(2,1)S(1)}, bf16[2,32,1280]{2,1,0:T(8,128)(2,1)S(1)}, u32[]{:S(2)}, u32[]{:S(2)}) collective-permute-start(bf16[2,32,1280]{2,1,0:T(8,128)(2,1)S(1)} %get-tuple-element.19), channel_id=1, source_target_pairs={{1,0},{2,1},{3,2},{4,3},{5,4},{6,5},{7,6},{8,7},{9,8},{10,9},{11,1... | collective-permute-start | bytes 491528 | tf_op jit(solution)/shard_map/ppermute | solution.py:24
  (2 other events, 27.5 us)

commit v2 on v1

--- a/solution.py
+++ b/solution.py
@@ -265,12 +265,11 @@
     partial = partial.astype(jnp.bfloat16)
     weight_grad = scattered_sum(partial)
 
-    group_attn = dot(group_grad, weight, 1, 1)
-    sent = group_attn.astype(jnp.bfloat16)
+    sent = dot(group_grad, weight, 1, 1).astype(jnp.bfloat16)
     here_other = flipped(sent[tokens : 2 * tokens], 0, 1)
     pair_own = flipped(sent[2 * tokens : 3 * tokens], 1, 0)
     pair_other = flipped(sent[3 * tokens :], 1, 1)
-    own_half = group_attn[:tokens] + pair_own.astype(jnp.float32)
+    own_half = sent[:tokens].astype(jnp.float32) + pair_own.astype(jnp.float32)
     other_half = here_other.astype(jnp.float32) + pair_other.astype(jnp.float32)
     split_attn = jnp.concatenate([own_half, other_half], axis=1).astype(jnp.bfloat16)
     grad_attn = dot(split_attn, picks, 1, 0).astype(jnp.bfloat16)

time: 177 us -> 172 us (0.972)
  the two profiles are of different devices: /device:TPU:15 before, /device:TPU:235 now
where the time goes in v2:
time: 172 us; the launch traced here: 171 us
  waiting for transfers between devices  73.4 us (43%)
  starting transfers between devices  58.4 us (34%)
  Pallas kernels  14.9 us (9%)
  matrix products  9.69 us (6%)
  other arithmetic  8.01 us (5%)
  local copies, waits for them, and re-layouts  5.37 us (3%)
    ppermute x8, waiting for transfers between devices, shifted(): lax.ppermute(value, axis, [(source, source + steps) for source in range(f...  43.6 us
    ppermute x8, waiting for transfers between devices, flipped(): return lax.ppermute(value, ('y', 'c'), pairs)  29.8 us
    ppermute x8, starting transfers between devices, shifted(): lax.ppermute(value, axis, [(source, source + steps) for source in range(f...  26 us
    all_to_all x4, starting transfers between devices, exchanged(): return lax.all_to_all(blocks, axis, 0, 0, tiled=True)  22.7 us
    dot_general x4, matrix products, dot(): lax.dot_general(a, b, (((a_dim,), (b_dim,)), ((), ())), preferred_element...  9.69 us
    ppermute x8, starting transfers between devices, flipped(): return lax.ppermute(value, ('y', 'c'), pairs)  9.65 us
    pallas_call x1, Pallas kernels, attention_grads(): pl.pallas_call(grads_kernel, grid=(inner // LANES // PER_STEP,), in_specs...  8.27 us
    pallas_call x1, Pallas kernels, attend(): pl.pallas_call(attend_kernel, grid=(inner // LANES // PER_STEP,), in_spec...  6.6 us
  transfers between devices with their start and end apart: 20, of which 8 were waited for; matrix products, arithmetic and copies ran while one was open for 12% of the time, Pallas kernels for 9%

profile of v2, /device:TPU:235, one launch (start us, length us, event | category | flops | bytes accessed | tf_op | source)
XLA Modules:
  0.0 170.8 jit_solution(7698673951240972327)
XLA Ops:
  3.2 4.8 %collective-permute-start.5 = (bf16[2,32,1280]{2,1,0:T(8,128)(2,1)S(1)}, bf16[2,32,1280]{2,1,0:T(8,128)(2,1)S(1)}, u32[]{:S(2)}, u32[]{:S(2)}) collective-permute-start(bf16[2,32,1280]{2,1,0:T(8,128)(2,1)S(1)} %get-tuple-element.22), channel_id=1, source_target_pairs={{0,1},{1,2},{2,3},{3,4},{4,5},{5,6},{6,7},{7,8},{8,9},{9,10},{10,1... | collective-permute-start | bytes 491528 | tf_op jit(solution)/shard_map/ppermute | solution.py:24
  10.7 5.3 %all-to-all-start = ((bf16[8,5,2560]{2,1,0:T(8,128)(2,1)}), bf16[8,5,2560]{2,1,0:T(8,128)(2,1)S(1)}, u32[]{:S(2)}, u32[]{:S(2)}) async-start(bf16[8,5,2560]{2,1,0:T(8,128)(2,1)} %broadcast_in_dim.24), calls=%async_computation | async-start | bytes 655360 | tf_op jit(solution)/shard_map/all_to_all | solution.py:28
  17.4 3.8 %collective-permute-start.7 = (bf16[2,192,1280]{2,1,0:T(8,128)(2,1)S(1)}, bf16[2,192,1280]{2,1,0:T(8,128)(2,1)}, u32[]{:S(2)}, u32[]{:S(2)}) collective-permute-start(bf16[2,192,1280]{2,1,0:T(8,128)(2,1)S(1)} %pad_maximum_fusion.1.refs_1_), channel_id=1, source_target_pairs={{0,16},{16,32},{32,48},{48,64},{64,80},{80,96},{96,112},{112,128},... | collective-permute-start | bytes 2949128 | tf_op jit(solution)/shard_map/ppermute | solution.py:24
  21.2 1.9 %collective-permute-start.8 = (bf16[2,192,1280]{2,1,0:T(8,128)(2,1)S(1)}, bf16[2,192,1280]{2,1,0:T(8,128)(2,1)}, u32[]{:S(2)}, u32[]{:S(2)}) collective-permute-start(bf16[2,192,1280]{2,1,0:T(8,128)(2,1)S(1)} %pad_maximum_fusion.1.refs_1_), channel_id=1, source_target_pairs={{16,0},{32,16},{48,32},{64,48},{80,64},{96,80},{112,96},{128,112},... | collective-permute-start | bytes 2949128 | tf_op jit(solution)/shard_map/ppermute | solution.py:24
  26.3 7.0 %all-to-all-start.1 = ((bf16[16,40,1280]{2,1,0:T(8,128)(2,1)}), bf16[16,40,1280]{2,1,0:T(8,128)(2,1)}, u32[]{:S(2)}, u32[]{:S(2)}) async-start(bf16[16,40,1280]{2,1,0:T(8,128)(2,1)} %bitcast.9), calls=%async_computation.1 | async-start | bytes 3276800 | tf_op jit(solution)/shard_map/all_to_all | solution.py:28
  34.4 3.6 %collective-permute-start.1 = (bf16[2,128,1280]{2,1,0:T(8,128)(2,1)S(1)}, bf16[2,128,1280]{2,1,0:T(8,128)(2,1)S(1)}, u32[]{:S(2)}, u32[]{:S(2)}) collective-permute-start(bf16[2,128,1280]{2,1,0:T(8,128)(2,1)S(1)} %get-tuple-element.28), channel_id=1, source_target_pairs={{0,1},{1,0},{4,5},{5,4},{8,9},{9,8},{12,13},{13,12},{2,3},{3,2},{6... | collective-permute-start | bytes 1966088 | tf_op jit(solution)/shard_map/ppermute | solution.py:36
  38.0 8.4 %collective-permute-done.7.refs_0_ = bf16[2,192,1280]{2,1,0:T(8,128)(2,1)} collective-permute-done((bf16[2,192,1280]{2,1,0:T(8,128)(2,1)S(1)}, bf16[2,192,1280]{2,1,0:T(8,128)(2,1)}, u32[]{:S(2)}, u32[]{:S(2)}) %collective-permute-start.7) | collective-permute-done | bytes 983072 | tf_op jit(solution)/shard_map/ppermute | solution.py:24
  46.4 3.8 %collective-permute-done.8.refs_2_ = bf16[2,192,1280]{2,1,0:T(8,128)(2,1)} collective-permute-done((bf16[2,192,1280]{2,1,0:T(8,128)(2,1)S(1)}, bf16[2,192,1280]{2,1,0:T(8,128)(2,1)}, u32[]{:S(2)}, u32[]{:S(2)}) %collective-permute-start.8) | collective-permute-done | bytes 983072 | tf_op jit(solution)/shard_map/ppermute | solution.py:24
  50.2 6.6 %attend.1 = (bf16[128,1280]{1,0:T(8,128)(2,1)}, f32[10,8,256]{2,1,0:T(8,128)}) custom-call(bf16[128,1280]{1,0:T(8,128)(2,1)} %bitcast.52, bf16[2,192,1280]{2,1,0:T(8,128)(2,1)} %collective-permute-done.7.refs_0_, bf16[2,192,1280]{2,1,0:T(8,128)(2,1)} %copy-done, bf16[2,192,1280]{2,1,0:T(8,128)(2,1)} %collective-permute-done.8.refs_2_, ...), custom_call_target="tpu_custom_call" | custom-call | flops 754974720 | bytes 2949120 | tf_op jit(solution)/shard_map/attend/pallas_call | solution.py:189
  56.8 2.5 %fusion.6 = bf16[128,1280]{1,0:T(8,128)(2,1)S(1)} fusion(bf16[128,1280]{1,0:T(8,128)(2,1)} %get-tuple-element.15, s32[1280]{0:T(1024)S(1)} %fusion.47), kind=kOutput, calls=%fused_computation.8 | convolution fusion | flops 421232640 | bytes 660480 | tf_op jit(solution)/shard_map/dot_general | solution.py:116
  62.0 9.8 %collective-permute-done.14 = bf16[128,640]{1,0:T(8,128)(2,1)S(1)} collective-permute-done((bf16[128,640]{1,0:T(8,128)(2,1)S(1)}, bf16[128,640]{1,0:T(8,128)(2,1)S(1)}, u32[]{:S(2)}, u32[]{:S(2)}) %collective-permute-start.14) | collective-permute-done | bytes 163872 | tf_op jit(solution)/shard_map/ppermute | solution.py:36
  71.8 2.2 %fusion.4 = bf16[640,1280]{1,0:T(8,128)(2,1)} fusion(bf16[512,1280]{1,0:T(8,128)(2,1)S(1)} %bitcast.41, bf16[128,640]{1,0:T(8,128)(2,1)S(1)} %collective-permute-done.15, bf16[128,640]{1,0:T(8,128)(2,1)S(1)} %collective-permute-done.14, bf16[128,640]{1,0:T(8,128)(2,1)S(1)} %collective-permute-done.13, bf16[128,640]{1,0:T(8,128)(2,1)S(1)} %get-tuple-element.31), kind=kOutput, calls=%fused_computation.6 | convolution fusion | flops 843120640 | bytes 3604480 | tf_op jit(solution)/shard_map/dot_general | solution.py:116
  74.1 6.4 %all-to-all-start.2 = ((bf16[16,40,1280]{2,1,0:T(8,128)(2,1)}), bf16[16,40,1280]{2,1,0:T(8,128)(2,1)S(1)}, u32[]{:S(2)}, u32[]{:S(2)}) async-start(bf16[16,40,1280]{2,1,0:T(8,128)(2,1)} %bitcast.20), calls=%async_computation.2 | async-start | bytes 3276800 | tf_op jit(solution)/shard_map/all_to_all | solution.py:28
  80.5 2.6 %convolution_convert_fusion = bf16[512,640]{1,0:T(8,128)(2,1)S(1)} fusion(bf16[512,1280]{1,0:T(8,128)(2,1)S(1)} %bitcast.42, bf16[640,1280]{1,0:T(8,128)(2,1)} %bitcast.10), kind=kOutput, calls=%fused_computation.10 | convolution fusion | flops 839188480 | bytes 3604480 | tf_op jit(solution)/shard_map/dot_general | solution.py:116
  86.5 15.7 %collective-permute-done.2 = bf16[128,640]{1,0:T(8,128)(2,1)S(1)} collective-permute-done((bf16[128,640]{1,0:T(8,128)(2,1)S(1)}, bf16[128,640]{1,0:T(8,128)(2,1)S(1)}, u32[]{:S(2)}, u32[]{:S(2)}) %collective-permute-start.2) | collective-permute-done | bytes 163872 | tf_op jit(solution)/shard_map/ppermute | solution.py:36
  102.3 4.3 %collective-permute-done.4 = bf16[128,640]{1,0:T(8,128)(2,1)S(1)} collective-permute-done((bf16[128,640]{1,0:T(8,128)(2,1)S(1)}, bf16[128,640]{1,0:T(8,128)(2,1)S(1)}, u32[]{:S(2)}, u32[]{:S(2)}) %collective-permute-start.4) | collective-permute-done | bytes 163872 | tf_op jit(solution)/shard_map/ppermute | solution.py:36
  106.6 2.3 %fusion.5.g_ref = bf16[128,1280]{1,0:T(8,128)(2,1)} fusion(s32[1280]{0:T(1024)S(1)} %fusion.47, bf16[128,640]{1,0:T(8,128)(2,1)S(1)} %add_convert_fusion, bf16[128,640]{1,0:T(8,128)(2,1)S(1)} %add_convert_fusion.1), kind=kOutput, calls=%fused_computation.7 | convolution fusion | flops 421888000 | bytes 660480 | tf_op jit(solution)/shard_map/dot_general | solution.py:116
  108.9 8.3 %attention_grads.1 = (bf16[128,1280]{1,0:T(8,128)(2,1)}, bf16[2,192,1280]{2,1,0:T(8,128)(2,1)}, bf16[2,192,1280]{2,1,0:T(8,128)(2,1)}, bf16[2,192,1280]{2,1,0:T(8,128)(2,1)}) custom-call(bf16[128,1280]{1,0:T(8,128)(2,1)} %bitcast.53, bf16[128,1280]{1,0:T(8,128)(2,1)} %fusion.5.g_ref, f32[10,8,256]{2,1,0:T(8,128)} %get-tuple-element.10.total_ref, ...), custom_call_target="tpu_custom_call" | custom-call | flops 1887436800 | bytes 5898240 | tf_op jit(solution)/shard_map/attention_grads/pallas_call | solution.py:209
  117.2 4.0 %collective-permute-start.10 = (bf16[2,192,1280]{2,1,0:T(8,128)(2,1)}, bf16[2,192,1280]{2,1,0:T(8,128)(2,1)}, u32[]{:S(2)}, u32[]{:S(2)}) collective-permute-start(bf16[2,192,1280]{2,1,0:T(8,128)(2,1)} %get-tuple-element.14), channel_id=1, source_target_pairs={{0,16},{16,32},{32,48},{48,64},{64,80},{80,96},{96,112},{112,128},... | collective-permute-start | bytes 2949128 | tf_op jit(solution)/shard_map/ppermute | solution.py:24
  124.3 4.0 %all-to-all-start.3 = ((bf16[8,5,2560]{2,1,0:T(8,128)(2,1)}), bf16[8,5,2560]{2,1,0:T(8,128)(2,1)S(1)}, u32[]{:S(2)}, u32[]{:S(2)}) async-start(bf16[8,5,2560]{2,1,0:T(8,128)(2,1)} %pad_maximum_fusion.3), calls=%async_computation.3 | async-start | bytes 655360 | tf_op jit(solution)/shard_map/all_to_all | solution.py:28
  128.2 18.3 %collective-permute-done.10 = bf16[2,192,1280]{2,1,0:T(8,128)(2,1)} collective-permute-done((bf16[2,192,1280]{2,1,0:T(8,128)(2,1)}, bf16[2,192,1280]{2,1,0:T(8,128)(2,1)}, u32[]{:S(2)}, u32[]{:S(2)}) %collective-permute-start.10) | collective-permute-done | bytes 983072 | tf_op jit(solution)/shard_map/ppermute | solution.py:24
  146.5 8.2 %collective-permute-done.9 = bf16[2,192,1280]{2,1,0:T(8,128)(2,1)} collective-permute-done((bf16[2,192,1280]{2,1,0:T(8,128)(2,1)}, bf16[2,192,1280]{2,1,0:T(8,128)(2,1)}, u32[]{:S(2)}, u32[]{:S(2)}) %collective-permute-start.9) | collective-permute-done | bytes 983072 | tf_op jit(solution)/shard_map/ppermute | solution.py:24
  156.6 5.7 %collective-permute-start.11 = (bf16[2,32,1280]{2,1,0:T(8,128)(2,1)S(1)}, bf16[2,32,1280]{2,1,0:T(8,128)(2,1)S(1)}, u32[]{:S(2)}, u32[]{:S(2)}) collective-permute-start(bf16[2,32,1280]{2,1,0:T(8,128)(2,1)S(1)} %get-tuple-element.18), channel_id=1, source_target_pairs={{0,1},{1,2},{2,3},{3,4},{4,5},{5,6},{6,7},{7,8},{8,9},{9,10},{10,1... | collective-permute-start | bytes 491528 | tf_op jit(solution)/shard_map/ppermute | solution.py:24
  165.0 4.9 %collective-permute-done.12 = bf16[2,32,1280]{2,1,0:T(8,128)(2,1)S(1)} collective-permute-done((bf16[2,32,1280]{2,1,0:T(8,128)(2,1)S(1)}, bf16[2,32,1280]{2,1,0:T(8,128)(2,1)S(1)}, u32[]{:S(2)}, u32[]{:S(2)}) %collective-permute-start.12) | collective-permute-done | bytes 163872 | tf_op jit(solution)/shard_map/ppermute | solution.py:24
  (84 shorter events, 25.2 us)
Async XLA Ops:
  0.7 15.5 %copy-start.5 = (s32[1,4,4,3]{2,1,3,0:T(4,128)S(1)}, s32[1,4,4,3]{2,1,3,0:T(4,128)}, u32[]{:S(2)}) copy-start(s32[1,4,4,3]{2,1,3,0:T(4,128)} %param.11) | copy-start | bytes 580
  0.7 16.6 %copy-start.1 = (bf16[1,4,32,1280]{3,2,1,0:T(8,128)(2,1)S(1)}, bf16[1,4,32,1280]{3,2,1,0:T(8,128)(2,1)}, u32[]{:S(2)}) copy-start(bf16[1,4,32,1280]{3,2,1,0:T(8,128)(2,1)} %param.8) | copy-start | bytes 983044
  0.7 16.6 %copy-start.2 = (bf16[1,4,32,1280]{3,2,1,0:T(8,128)(2,1)S(1)}, bf16[1,4,32,1280]{3,2,1,0:T(8,128)(2,1)}, u32[]{:S(2)}) copy-start(bf16[1,4,32,1280]{3,2,1,0:T(8,128)(2,1)} %param.7) | copy-start | bytes 983044
  1.9 31.4 %collective-permute-start = (bf16[128,1280]{1,0:T(8,128)(2,1)S(1)}, bf16[128,1280]{1,0:T(8,128)(2,1)}, u32[]{:S(2)}, u32[]{:S(2)}) collective-permute-start(bf16[128,1280]{1,0:T(8,128)(2,1)S(1)} %get-tuple-element.30), channel_id=1, source_target_pairs={{0,4},{1,5},{4,0},{5,1},{8,12},{9,13},{12,8},{13,9},{2,6},{3,7},{6... | collective-permute-start | bytes 983048 | tf_op jit(solution)/shard_map/ppermute | solution.py:36
  3.2 14.1 %collective-permute-start.5 = (bf16[2,32,1280]{2,1,0:T(8,128)(2,1)S(1)}, bf16[2,32,1280]{2,1,0:T(8,128)(2,1)S(1)}, u32[]{:S(2)}, u32[]{:S(2)}) collective-permute-start(bf16[2,32,1280]{2,1,0:T(8,128)(2,1)S(1)} %get-tuple-element.22), channel_id=1, source_target_pairs={{0,1},{1,2},{2,3},{3,4},{4,5},{5,6},{6,7},{7,8},{8,9},{9,10},{10,1... | collective-permute-start | bytes 491528 | tf_op jit(solution)/shard_map/ppermute | solution.py:24
  8.0 9.3 %collective-permute-start.6 = (bf16[2,32,1280]{2,1,0:T(8,128)(2,1)S(1)}, bf16[2,32,1280]{2,1,0:T(8,128)(2,1)S(1)}, u32[]{:S(2)}, u32[]{:S(2)}) collective-permute-start(bf16[2,32,1280]{2,1,0:T(8,128)(2,1)S(1)} %get-tuple-element.23), channel_id=1, source_target_pairs={{1,0},{2,1},{3,2},{4,3},{5,4},{6,5},{7,6},{8,7},{9,8},{10,9},{11,1... | collective-permute-start | bytes 491528 | tf_op jit(solution)/shard_map/ppermute | solution.py:24
  10.7 14.1 %all-to-all-start = ((bf16[8,5,2560]{2,1,0:T(8,128)(2,1)}), bf16[8,5,2560]{2,1,0:T(8,128)(2,1)S(1)}, u32[]{:S(2)}, u32[]{:S(2)}) async-start(bf16[8,5,2560]{2,1,0:T(8,128)(2,1)} %broadcast_in_dim.24), calls=%async_computation | async-start | bytes 655360 | tf_op jit(solution)/shard_map/all_to_all | solution.py:28
  17.4 29.0 %collective-permute-start.7 = (bf16[2,192,1280]{2,1,0:T(8,128)(2,1)S(1)}, bf16[2,192,1280]{2,1,0:T(8,128)(2,1)}, u32[]{:S(2)}, u32[]{:S(2)}) collective-permute-start(bf16[2,192,1280]{2,1,0:T(8,128)(2,1)S(1)} %pad_maximum_fusion.1.refs_1_), channel_id=1, source_target_pairs={{0,16},{16,32},{32,48},{48,64},{64,80},{80,96},{96,112},{112,128},... | collective-permute-start | bytes 2949128 | tf_op jit(solution)/shard_map/ppermute | solution.py:24
  21.2 29.0 %collective-permute-start.8 = (bf16[2,192,1280]{2,1,0:T(8,128)(2,1)S(1)}, bf16[2,192,1280]{2,1,0:T(8,128)(2,1)}, u32[]{:S(2)}, u32[]{:S(2)}) collective-permute-start(bf16[2,192,1280]{2,1,0:T(8,128)(2,1)S(1)} %pad_maximum_fusion.1.refs_1_), channel_id=1, source_target_pairs={{16,0},{32,16},{48,32},{64,48},{80,64},{96,80},{112,96},{128,112},... | collective-permute-start | bytes 2949128 | tf_op jit(solution)/shard_map/ppermute | solution.py:24
  26.3 47.8 %all-to-all-start.1 = ((bf16[16,40,1280]{2,1,0:T(8,128)(2,1)}), bf16[16,40,1280]{2,1,0:T(8,128)(2,1)}, u32[]{:S(2)}, u32[]{:S(2)}) async-start(bf16[16,40,1280]{2,1,0:T(8,128)(2,1)} %bitcast.9), calls=%async_computation.1 | async-start | bytes 3276800 | tf_op jit(solution)/shard_map/all_to_all | solution.py:28
  34.4 27.5 %collective-permute-start.1 = (bf16[2,128,1280]{2,1,0:T(8,128)(2,1)S(1)}, bf16[2,128,1280]{2,1,0:T(8,128)(2,1)S(1)}, u32[]{:S(2)}, u32[]{:S(2)}) collective-permute-start(bf16[2,128,1280]{2,1,0:T(8,128)(2,1)S(1)} %get-tuple-element.28), channel_id=1, source_target_pairs={{0,1},{1,0},{4,5},{5,4},{8,9},{9,8},{12,13},{13,12},{2,3},{3,2},{6... | collective-permute-start | bytes 1966088 | tf_op jit(solution)/shard_map/ppermute | solution.py:36
  59.3 2.7 %collective-permute-start.13 = (bf16[128,640]{1,0:T(8,128)(2,1)S(1)}, bf16[128,640]{1,0:T(8,128)(2,1)S(1)}, u32[]{:S(2)}, u32[]{:S(2)}) collective-permute-start(bf16[128,640]{1,0:T(8,128)(2,1)S(1)} %get-tuple-element.32), channel_id=1, source_target_pairs={{0,1},{1,0},{4,5},{5,4},{8,9},{9,8},{12,13},{13,12},{2,3},{3,2},{6... | collective-permute-start | bytes 491528 | tf_op jit(solution)/shard_map/ppermute | solution.py:36
  60.4 11.4 %collective-permute-start.15 = (bf16[128,640]{1,0:T(8,128)(2,1)S(1)}, bf16[128,640]{1,0:T(8,128)(2,1)S(1)}, u32[]{:S(2)}, u32[]{:S(2)}) collective-permute-start(bf16[128,640]{1,0:T(8,128)(2,1)S(1)} %get-tuple-element.32), channel_id=1, source_target_pairs={{0,5},{1,4},{4,1},{5,0},{8,13},{9,12},{12,9},{13,8},{2,7},{3,6},{6... | collective-permute-start | bytes 491528 | tf_op jit(solution)/shard_map/ppermute | solution.py:36
  60.4 11.4 %collective-permute-start.14 = (bf16[128,640]{1,0:T(8,128)(2,1)S(1)}, bf16[128,640]{1,0:T(8,128)(2,1)S(1)}, u32[]{:S(2)}, u32[]{:S(2)}) collective-permute-start(bf16[128,640]{1,0:T(8,128)(2,1)S(1)} %get-tuple-element.31), channel_id=1, source_target_pairs={{0,4},{1,5},{4,0},{5,1},{8,12},{9,13},{12,8},{13,9},{2,6},{3,7},{6... | collective-permute-start | bytes 491528 | tf_op jit(solution)/shard_map/ppermute | solution.py:36
  74.1 49.0 %all-to-all-start.2 = ((bf16[16,40,1280]{2,1,0:T(8,128)(2,1)}), bf16[16,40,1280]{2,1,0:T(8,128)(2,1)S(1)}, u32[]{:S(2)}, u32[]{:S(2)}) async-start(bf16[16,40,1280]{2,1,0:T(8,128)(2,1)} %bitcast.20), calls=%async_computation.2 | async-start | bytes 3276800 | tf_op jit(solution)/shard_map/all_to_all | solution.py:28
  83.2 19.0 %collective-permute-start.2 = (bf16[128,640]{1,0:T(8,128)(2,1)S(1)}, bf16[128,640]{1,0:T(8,128)(2,1)S(1)}, u32[]{:S(2)}, u32[]{:S(2)}) collective-permute-start(bf16[128,640]{1,0:T(8,128)(2,1)S(1)} %get-tuple-element.24), channel_id=1, source_target_pairs={{0,4},{1,5},{4,0},{5,1},{8,12},{9,13},{12,8},{13,9},{2,6},{3,7},{6... | collective-permute-start | bytes 491528 | tf_op jit(solution)/shard_map/ppermute | solution.py:36
  83.6 18.7 %collective-permute-start.3 = (bf16[128,640]{1,0:T(8,128)(2,1)S(1)}, bf16[128,640]{1,0:T(8,128)(2,1)S(1)}, u32[]{:S(2)}, u32[]{:S(2)}) collective-permute-start(bf16[128,640]{1,0:T(8,128)(2,1)S(1)} %get-tuple-element.26), channel_id=1, source_target_pairs={{0,1},{1,0},{4,5},{5,4},{8,9},{9,8},{12,13},{13,12},{2,3},{3,2},{6... | collective-permute-start | bytes 491528 | tf_op jit(solution)/shard_map/ppermute | solution.py:36
  85.4 21.1 %collective-permute-start.4 = (bf16[128,640]{1,0:T(8,128)(2,1)S(1)}, bf16[128,640]{1,0:T(8,128)(2,1)S(1)}, u32[]{:S(2)}, u32[]{:S(2)}) collective-permute-start(bf16[128,640]{1,0:T(8,128)(2,1)S(1)} %get-tuple-element.25), channel_id=1, source_target_pairs={{0,5},{1,4},{4,1},{5,0},{8,13},{9,12},{12,9},{13,8},{2,7},{3,6},{6... | collective-permute-start | bytes 491528 | tf_op jit(solution)/shard_map/ppermute | solution.py:36
  117.2 29.4 %collective-permute-start.10 = (bf16[2,192,1280]{2,1,0:T(8,128)(2,1)}, bf16[2,192,1280]{2,1,0:T(8,128)(2,1)}, u32[]{:S(2)}, u32[]{:S(2)}) collective-permute-start(bf16[2,192,1280]{2,1,0:T(8,128)(2,1)} %get-tuple-element.14), channel_id=1, source_target_pairs={{0,16},{16,32},{32,48},{48,64},{64,80},{80,96},{96,112},{112,128},... | collective-permute-start | bytes 2949128 | tf_op jit(solution)/shard_map/ppermute | solution.py:24
  121.2 33.5 %collective-permute-start.9 = (bf16[2,192,1280]{2,1,0:T(8,128)(2,1)}, bf16[2,192,1280]{2,1,0:T(8,128)(2,1)}, u32[]{:S(2)}, u32[]{:S(2)}) collective-permute-start(bf16[2,192,1280]{2,1,0:T(8,128)(2,1)} %get-tuple-element.13), channel_id=1, source_target_pairs={{16,0},{32,16},{48,32},{64,48},{80,64},{96,80},{112,96},{128,112},... | collective-permute-start | bytes 2949128 | tf_op jit(solution)/shard_map/ppermute | solution.py:24
  123.1 31.6 %copy-start.3 = (bf16[2,192,1280]{2,1,0:T(8,128)(2,1)S(1)}, bf16[2,192,1280]{2,1,0:T(8,128)(2,1)}, u32[]{:S(2)}) copy-start(bf16[2,192,1280]{2,1,0:T(8,128)(2,1)} %get-tuple-element.12) | copy-start | bytes 2949124
  124.3 40.0 %all-to-all-start.3 = ((bf16[8,5,2560]{2,1,0:T(8,128)(2,1)}), bf16[8,5,2560]{2,1,0:T(8,128)(2,1)S(1)}, u32[]{:S(2)}, u32[]{:S(2)}) async-start(bf16[8,5,2560]{2,1,0:T(8,128)(2,1)} %pad_maximum_fusion.3), calls=%async_computation.3 | async-start | bytes 655360 | tf_op jit(solution)/shard_map/all_to_all | solution.py:28
  156.6 8.4 %collective-permute-start.11 = (bf16[2,32,1280]{2,1,0:T(8,128)(2,1)S(1)}, bf16[2,32,1280]{2,1,0:T(8,128)(2,1)S(1)}, u32[]{:S(2)}, u32[]{:S(2)}) collective-permute-start(bf16[2,32,1280]{2,1,0:T(8,128)(2,1)S(1)} %get-tuple-element.18), channel_id=1, source_target_pairs={{0,1},{1,2},{2,3},{3,4},{4,5},{5,6},{6,7},{7,8},{8,9},{9,10},{10,1... | collective-permute-start | bytes 491528 | tf_op jit(solution)/shard_map/ppermute | solution.py:24
  162.3 7.5 %collective-permute-start.12 = (bf16[2,32,1280]{2,1,0:T(8,128)(2,1)S(1)}, bf16[2,32,1280]{2,1,0:T(8,128)(2,1)S(1)}, u32[]{:S(2)}, u32[]{:S(2)}) collective-permute-start(bf16[2,32,1280]{2,1,0:T(8,128)(2,1)S(1)} %get-tuple-element.19), channel_id=1, source_target_pairs={{1,0},{2,1},{3,2},{4,3},{5,4},{6,5},{7,6},{8,7},{9,8},{10,9},{11,1... | collective-permute-start | bytes 491528 | tf_op jit(solution)/shard_map/ppermute | solution.py:24
  (2 other events, 18.2 us)
